TPU v7x, 32 devices: a whole 2x2x4 slice. The times are simulated.
32 devices in a mesh: rows: 8 (over z, y), cols: 4 (over x, core).
Axes of the slice: x: 2, y: 2, z: 4, core: 2. Of those that a mesh axis runs over, the one named last changes fastest.
Arguments:
- tiles: bfloat16 [2, 8, 4, 128, 128, 128], P(None, 'rows', 'cols'), may hold values from -0.15625 to 0.15625
- tile_scales: float32 [2, 8, 4, 128], P(None, 'rows', 'cols'), may hold values from 0.5 to 4
- tile_rows: int32 [2, 8, 4, 128], P(None, 'rows', 'cols'), may hold values from 0 to 7
- tile_cols: int32 [2, 8, 4, 128], P(None, 'rows', 'cols'), may hold values from 0 to 1023
- tile_counts: int32 [2, 8, 4], P(None, 'rows', 'cols'), may hold values from 32 to 128, as said below
- labels: int32 [2, 8192], P(None, 'rows'), may hold values from 0 to 31
- learning_rate: float32 [2], replicated, may hold values from 4 to 16
- weights: float32 [32, 524288], P(None, ('cols', 'rows')), may hold values from -6 to 6
Outputs:
- trained: float32 [32, 524288], P(None, ('cols', 'rows'))
- losses: float32 [2, 8192], P(None, ('rows', 'cols'))
Inputs may be any that keep to these rules, and one draw needn't show every extreme that they name: Only the first tile_counts[s, r, c] slots of a block are live; in every step some block has all 128 slots live.
All inputs are finite; a program needn't handle non-finite values.
Results may differ from a plain program's by a relative error of at most 0.0021.
Values may be sent and summed in bfloat16 or wider, within the bound.
A program may use at most 128 MiB of HBM per device.

v0:
```python
import functools
import math
import jax
import jax.numpy as jnp
from jax import lax
from jax.experimental import pallas as pl
from jax.experimental.pallas import tpu as pltpu
from jax.sharding import PartitionSpec as P

MESH = pl.DeviceIdType.MESH
VMEM_LIMIT = 48 * 1024 * 1024
VM = pl.BlockSpec(memory_space=pltpu.VMEM)
SM = pl.BlockSpec(memory_space=pltpu.SMEM)
LOCAL = pltpu.CompilerParams(vmem_limit_bytes=VMEM_LIMIT)
SLOTS = pltpu.CompilerParams(vmem_limit_bytes=48 * 1024 * 1024)


def lanes(block, size):
    return pl.ds(pl.multiple_of(block * size, size), size)


def pack_body(size, step, capacity, requests_ref, weights_ref, send_ref):
    owners = send_ref.shape[0] // capacity
    full = requests_ref.shape[1] // owners

    @pl.loop(0, capacity)
    def _(index):
        for peer in range(owners):
            where = lanes(requests_ref[step, peer * full + index], size)
            send_ref[peer * capacity + index] = weights_ref[:, where].astype(jnp.bfloat16)


def apply_body(size, step, capacity, requests_ref, rate_ref, weights_ref, grads_ref, out_ref):
    owners = grads_ref.shape[0] // capacity
    full = requests_ref.shape[1] // owners
    out_ref[...] = weights_ref[...]
    rate = rate_ref[step]

    @pl.loop(0, capacity)
    def _(index):
        for peer in range(owners):
            where = lanes(requests_ref[step, peer * full + index], size)
            grad = grads_ref[peer * capacity + index].astype(jnp.float32)
            out_ref[:, where] -= rate * grad


def apply_kernel(size, step, capacity, requests_ref, rate_ref, weights_ref, grads_ref, out_ref):
    apply_body(size, step, capacity, requests_ref, rate_ref, weights_ref, grads_ref, out_ref)


def apply_pack_kernel(
    size, step, capacity, requests_ref, rate_ref, weights_ref, grads_ref, out_ref, send_ref
):
    apply_body(size, step, capacity, requests_ref, rate_ref, weights_ref, grads_ref, out_ref)
    pack_body(size, step + 1, capacity, requests_ref, out_ref, send_ref)


def exchange_kernel(axis, count, send_ref, recv_ref, send_sems, recv_sems, own_sem):
    me = lax.axis_index(axis)
    barrier = pltpu.get_barrier_semaphore()
    for shift in range(1, count):
        peer = lax.rem(me + shift, count)
        pl.semaphore_signal(barrier, inc=1, device_id={axis: peer}, device_id_type=MESH)
    own = pltpu.make_async_copy(send_ref.at[me], recv_ref.at[me], own_sem)
    own.start()
    pl.semaphore_wait(barrier, count - 1)
    copies = []
    for shift in sorted(range(1, count), key=lambda shift: abs(2 * shift - count)):
        peer = lax.rem(me + shift, count)
        copy = pltpu.make_async_remote_copy(
            src_ref=send_ref.at[peer],
            dst_ref=recv_ref.at[me],
            send_sem=send_sems.at[shift],
            recv_sem=recv_sems.at[shift],
            device_id={axis: peer},
            device_id_type=MESH,
        )
        copy.start()
        copies.append(copy)
    own.wait()
    for copy in copies:
        copy.wait()


def exchange(send, axis, count, collective_id):
    return pl.pallas_call(
        functools.partial(exchange_kernel, axis, count),
        out_shape=jax.ShapeDtypeStruct(send.shape, send.dtype),
        in_specs=[VM],
        out_specs=VM,
        scratch_shapes=[
            pltpu.SemaphoreType.DMA((count,)),
            pltpu.SemaphoreType.DMA((count,)),
            pltpu.SemaphoreType.DMA,
        ],
        compiler_params=pltpu.CompilerParams(
            collective_id=collective_id, has_side_effects=True, vmem_limit_bytes=VMEM_LIMIT
        ),
        name="exchange",
    )(send)


def collect_kernel(n_rows, n_cols, mine_ref, all_ref, send_sems, recv_sems, own_sem):
    row, col = lax.axis_index("rows"), lax.axis_index("cols")
    row_peers = [lax.rem(row + shift, n_rows) for shift in range(1, n_rows)]
    col_peers = [lax.rem(col + shift, n_cols) for shift in range(1, n_cols)]
    barrier = pltpu.get_barrier_semaphore()
    for peer in row_peers:
        pl.semaphore_signal(barrier, inc=1, device_id={"rows": peer}, device_id_type=MESH)
    for peer in col_peers:
        pl.semaphore_signal(barrier, inc=1, device_id={"cols": peer}, device_id_type=MESH)
    own = pltpu.make_async_copy(mine_ref, all_ref.at[col, row], own_sem)
    own.start()
    pl.semaphore_wait(barrier, n_rows + n_cols - 2)
    copies = []
    for index, peer in enumerate(row_peers):
        copies.append(
            pltpu.make_async_remote_copy(
                src_ref=mine_ref,
                dst_ref=all_ref.at[col, row],
                send_sem=send_sems.at[index],
                recv_sem=recv_sems.at[index],
                device_id={"rows": peer},
                device_id_type=MESH,
            )
        )
        copies[-1].start()
    own.wait()
    for copy in copies:
        copy.wait()
    copies = []
    for index, peer in enumerate(col_peers):
        copies.append(
            pltpu.make_async_remote_copy(
                src_ref=all_ref.at[col],
                dst_ref=all_ref.at[col],
                send_sem=send_sems.at[n_rows + index],
                recv_sem=recv_sems.at[n_rows + index],
                device_id={"cols": peer},
                device_id_type=MESH,
            )
        )
        copies[-1].start()
    for copy in copies:
        copy.wait()


def collect(mine, n_rows, n_cols):
    return pl.pallas_call(
        functools.partial(collect_kernel, n_rows, n_cols),
        out_shape=jax.ShapeDtypeStruct((n_cols, n_rows, *mine.shape), mine.dtype),
        in_specs=[VM],
        out_specs=VM,
        scratch_shapes=[
            pltpu.SemaphoreType.DMA((n_rows + n_cols,)),
            pltpu.SemaphoreType.DMA((n_rows + n_cols,)),
            pltpu.SemaphoreType.DMA,
        ],
        compiler_params=pltpu.CompilerParams(collective_id=0, has_side_effects=True),
        name="collect",
    )(mine)


GROUP = 16


def slot_scalars(step, place_of, slot, code_ref, row_ref, scale_ref, count_ref):
    place = place_of(code_ref[step, slot])
    factor = jnp.where(slot < count_ref[step, 0, 0], scale_ref[step, 0, 0, slot], 0.0)
    return place, row_ref[step, 0, 0, slot], factor


def fetch_tiles(step, tiles_ref, held_ref, sems):
    def copy(group):
        part = pl.ds(group * GROUP, GROUP)
        return pltpu.make_async_copy(
            tiles_ref.at[step, 0, 0, part], held_ref.at[part], sems.at[group]
        )

    for group in range(held_ref.shape[0] // GROUP):
        copy(group).start()
    return lambda group: copy(group).wait()


def scores_kernel(
    step, place_of, code_ref, row_ref, scale_ref, count_ref, recv_ref, tiles_ref, out_ref,
    held_ref, sems,
):
    size = held_ref.shape[-1]
    arrived = fetch_tiles(step, tiles_ref, held_ref, sems)
    out_ref[...] = jnp.zeros_like(out_ref)

    @pl.loop(0, held_ref.shape[0] // GROUP)
    def _(group):
        arrived(group)
        products = []
        for lane in range(GROUP):
            slot = group * GROUP + lane
            place, row, factor = slot_scalars(
                step, place_of, slot, code_ref, row_ref, scale_ref, count_ref
            )
            product = lax.dot_general(
                recv_ref[place],
                held_ref[slot],
                (((1,), (1,)), ((), ())),
                preferred_element_type=jnp.float32,
            )
            products.append((row, product * factor))
        for row, product in products:
            out_ref[:, lanes(row, size)] += product


def classify_kernel(
    axis, count, step, part_ref, labels_ref, residual_ref, loss_ref, held, losses, send_sems,
    recv_sems,
):
    me = lax.axis_index(axis)
    barrier = pltpu.get_barrier_semaphore()
    for shift in range(1, count):
        peer = lax.rem(me + shift, count)
        pl.semaphore_signal(barrier, inc=1, device_id={axis: peer}, device_id_type=MESH)
    pl.semaphore_wait(barrier, count - 1)
    copies = []
    for shift in range(1, count):
        peer = lax.rem(me + shift, count)
        copy = pltpu.make_async_remote_copy(
            src_ref=part_ref,
            dst_ref=held.at[shift],
            send_sem=send_sems.at[shift],
            recv_sem=recv_sems.at[shift],
            device_id={axis: peer},
            device_id_type=MESH,
        )
        copy.start()
        copies.append(copy)
    scores = part_ref[...]
    for shift, copy in enumerate(copies):
        copy.wait()
        scores = scores + held[shift + 1]
    exp_scores = jnp.exp(scores)
    total = jnp.sum(exp_scores, axis=0, keepdims=True)
    class_ids = lax.broadcasted_iota(jnp.int32, scores.shape, 0)
    onehot = (class_ids == labels_ref[step : step + 1, :]).astype(jnp.float32)
    losses[...] = jnp.log(total) - jnp.sum(onehot * scores, axis=0, keepdims=True)
    if loss_ref.shape == losses.shape:
        loss_ref[...] = losses[...]
    else:
        loss_ref[...] = losses[:, lanes(me, loss_ref.shape[1])]
    residual_ref[...] = (exp_scores / total - onehot).astype(jnp.bfloat16)


def classify(step, n_cols, part, labels):
    classes, samples = part.shape
    owned = samples // n_cols
    return pl.pallas_call(
        functools.partial(classify_kernel, "cols", n_cols, step),
        out_shape=(
            jax.ShapeDtypeStruct((classes, samples), jnp.bfloat16),
            jax.ShapeDtypeStruct((1, owned if owned % 128 == 0 else samples), jnp.float32),
        ),
        in_specs=[VM, VM],
        out_specs=(VM, VM),
        scratch_shapes=[
            pltpu.VMEM((n_cols, classes, samples), jnp.float32),
            pltpu.VMEM((1, samples), jnp.float32),
            pltpu.SemaphoreType.DMA((n_cols,)),
            pltpu.SemaphoreType.DMA((n_cols,)),
        ],
        compiler_params=pltpu.CompilerParams(collective_id=1 + step, has_side_effects=True),
        name="classify",
    )(part, labels)


def grads_kernel(
    step, place_of, code_ref, row_ref, scale_ref, count_ref, residual_ref, tiles_ref,
    out_ref, total, held_ref, sems,
):
    size = held_ref.shape[-1]
    arrived = fetch_tiles(step, tiles_ref, held_ref, sems)
    total[...] = jnp.zeros_like(total)

    @pl.loop(0, held_ref.shape[0] // GROUP)
    def _(group):
        arrived(group)
        products = []
        for lane in range(GROUP):
            slot = group * GROUP + lane
            place, row, factor = slot_scalars(
                step, place_of, slot, code_ref, row_ref, scale_ref, count_ref
            )
            product = jnp.dot(
                residual_ref[:, lanes(row, size)],
                held_ref[slot],
                preferred_element_type=jnp.float32,
            )
            products.append((place, product * factor))
        for place, product in products:
            total[place] += product

    out_ref[...] = total[...].astype(jnp.bfloat16)


def sparse_program(
    capacity, branch, code, requests,
    tiles, tile_scales, tile_rows, tile_cols, tile_counts, labels, learning_rate, weights
):
    classes = weights.shape[0]
    size = tiles.shape[-1]
    steps = tiles.shape[0]
    n_rows, n_cols = lax.axis_size("rows"), lax.axis_size("cols")
    full = requests.shape[1] // n_rows
    samples = labels.shape[1]
    entries = n_rows * capacity
    packed = jax.ShapeDtypeStruct((entries, classes, size), jnp.bfloat16)
    owned = samples // n_cols
    scalars = (code, tile_rows, tile_scales, tile_counts)
    trade_id = 1 + steps + branch
    slots = tiles.shape[3]
    in_hbm = pl.BlockSpec(memory_space=pltpu.HBM)
    tile_room = [pltpu.VMEM(tiles.shape[3:], tiles.dtype), pltpu.SemaphoreType.DMA((slots // GROUP,))]

    def place_of(x):
        return x // full * capacity + lax.rem(x, full)

    def trade(x):
        blocks = x.reshape(n_rows, capacity, classes, size)
        return exchange(blocks, "rows", n_rows, trade_id).reshape(packed.shape)

    current = weights
    send = pl.pallas_call(
        functools.partial(pack_body, size, 0, capacity),
        out_shape=packed, in_specs=[SM, VM], out_specs=VM, compiler_params=LOCAL, name="pack",
    )(requests, current)
    losses = []
    for step in range(steps):
        got = trade(send)
        part = pl.pallas_call(
            functools.partial(scores_kernel, step, place_of),
            out_shape=jax.ShapeDtypeStruct((classes, samples), jnp.float32),
            in_specs=[SM] * 4 + [VM, in_hbm], out_specs=VM, compiler_params=SLOTS,
            scratch_shapes=tile_room, name="scores",
        )(*scalars, got, tiles)
        residual, loss = classify(step, n_cols, part, labels)
        if owned % 128 != 0:
            start = lax.axis_index("cols") * owned
            loss = lax.dynamic_slice_in_dim(loss, start, owned, axis=1)
        losses.append(loss)
        grads = pl.pallas_call(
            functools.partial(grads_kernel, step, place_of),
            out_shape=packed,
            in_specs=[SM] * 4 + [VM, in_hbm], out_specs=VM, compiler_params=SLOTS,
            scratch_shapes=[pltpu.VMEM((entries, classes, size), jnp.float32), *tile_room],
            name="grads",
        )(*scalars, residual, tiles)
        grads = trade(grads)
        shape = jax.ShapeDtypeStruct(current.shape, current.dtype)
        more = step + 1 < steps
        current, *send = pl.pallas_call(
            functools.partial(apply_pack_kernel if more else apply_kernel, size, step, capacity),
            out_shape=(shape, packed) if more else (shape,),
            in_specs=[SM, SM, VM, VM], out_specs=(VM, VM) if more else (VM,),
            compiler_params=LOCAL, name="apply",
        )(requests, learning_rate, current, grads)
        send = send[0] if more else None
    return current, jnp.concatenate(losses)


def per_device(
    tiles, tile_scales, tile_rows, tile_cols, tile_counts, labels, learning_rate, weights
):
    args = (tiles, tile_scales, tile_rows, tile_cols, tile_counts, labels, learning_rate, weights)
    size, slots = tiles.shape[-1], tiles.shape[3]
    n_rows, n_cols = lax.axis_size("rows"), lax.axis_size("cols")
    per_owner = weights.shape[1] // size
    full = min(per_owner, slots)
    mean = slots / n_rows
    tiers = [math.ceil(mean + spread * math.sqrt(mean)) for spread in (1.75, 2, 2.25, 2.5, 3, 4)]
    tiers = sorted({min(tier, full) for tier in tiers} | {full})
    slot_ids = jnp.arange(slots, dtype=jnp.int32)

    live = slot_ids < tile_counts[:, 0, 0, None]
    mine = jnp.where(live, tile_cols[:, 0, 0], -1)
    owner = jnp.where(live, mine // per_owner, -1)
    same = mine[:, :, None] == mine[:, None, :]
    before = slot_ids[:, None] > slot_ids[None, :]
    fresh = live & ~jnp.any(same & before, axis=-1)
    lower = (owner[:, :, None] == owner[:, None, :]) & (mine[:, None, :] < mine[:, :, None])
    rank = jnp.sum((lower & fresh[:, None, :]).astype(jnp.int32), axis=-1)
    code = jnp.where(live, owner * full + rank, 0)
    everyone = collect(jnp.where(fresh, mine * full + rank, -1), n_rows, n_cols)
    most = jnp.max(jnp.where(everyone >= 0, everyone % full, 0)) + 1

    row, col = lax.axis_index("rows"), lax.axis_index("cols")
    peers = lax.dynamic_index_in_dim(everyone, col, 0, keepdims=False)
    local = peers // full - row * per_owner
    asked = (peers >= 0) & (local >= 0) & (local < per_owner)
    order = jnp.where(asked, peers % full, -1)
    picks = order[..., None, :] == jnp.arange(full, dtype=jnp.int32)[:, None]
    wanted = jnp.sum(jnp.where(picks, local[..., None, :], 0), axis=-1)
    requests = jnp.swapaxes(wanted, 0, 1).reshape(-1, n_rows * full)

    def at_capacity(capacity, branch):
        return functools.partial(sparse_program, capacity, branch)

    branches = [at_capacity(capacity, branch) for branch, capacity in enumerate(tiers)]
    operands = (code, requests, *args)
    if len(branches) == 1:
        return branches[0](*operands)
    chosen = sum((most > tier).astype(jnp.int32) for tier in tiers[:-1])
    return lax.switch(chosen, branches, *operands)


SPILL = 12
TIERS = ((23, 14), (24, 16), (26, 18), (28, 22))
LEFT_RIGHT = (((1,), (1,)), ((), ()))


def teams(n_rows):
    team = n_rows // 2
    row = lax.axis_index("rows")
    half, place = row // team, lax.rem(row, team)
    mate = lambda shift: half * team + lax.rem(place + shift, team)
    other = lambda shift: (1 - half) * team + lax.rem(place + shift, team)
    return team, row, half, place, mate, other


def greet_rows(peers):
    barrier = pltpu.get_barrier_semaphore()
    for peer in peers:
        pl.semaphore_signal(barrier, inc=1, device_id={"rows": peer}, device_id_type=MESH)
    return lambda: pl.semaphore_wait(barrier, len(peers))


def slots_of(tile_cols, count, steps):
    slots = tile_cols.shape[1]
    ids = lax.broadcasted_iota(jnp.int32, (1, slots), 1)
    return [(tile_cols[s : s + 1, :], ids < count(s)) for s in range(steps)]


def mark_kernel(n_rows, n_cols, steps, cols_ref, count_ref, all_ref, mine, send_sems, recv_sems, own_sem):
    row, col = lax.axis_index("rows"), lax.axis_index("cols")
    row_peers = [lax.rem(row + shift, n_rows) for shift in range(1, n_rows)]
    col_peers = [lax.rem(col + shift, n_cols) for shift in range(1, n_cols)]
    barrier = pltpu.get_barrier_semaphore()
    for peer in row_peers:
        pl.semaphore_signal(barrier, inc=1, device_id={"rows": peer}, device_id_type=MESH)
    for peer in col_peers:
        pl.semaphore_signal(barrier, inc=1, device_id={"cols": peer}, device_id_type=MESH)
    size = mine.shape[1]
    marks = []
    for cols, live in slots_of(cols_ref[...], lambda s: count_ref[s, 0, 0], steps):
        slots = cols.shape[1]
        owners = lax.broadcasted_iota(jnp.int32, (n_rows, slots), 0)
        places = lax.broadcasted_iota(jnp.int32, (size, slots), 0)
        first = jnp.where(live & (cols >> 7 == owners), 1.0, 0.0).astype(jnp.bfloat16)
        second = jnp.where((cols & 127) == places, 1.0, 0.0).astype(jnp.bfloat16)
        count = lax.dot_general(first, second, LEFT_RIGHT, preferred_element_type=jnp.float32)
        marks.append(jnp.minimum(count, 1.0))
    mine[...] = jnp.concatenate(marks, axis=0).astype(jnp.bfloat16)
    pl.semaphore_wait(barrier, n_rows + n_cols - 2)
    own = pltpu.make_async_copy(mine, all_ref.at[col, row], own_sem)
    own.start()
    copies = []
    for index, peer in enumerate(row_peers):
        copies.append(
            pltpu.make_async_remote_copy(
                src_ref=mine,
                dst_ref=all_ref.at[col, row],
                send_sem=send_sems.at[index],
                recv_sem=recv_sems.at[index],
                device_id={"rows": peer},
                device_id_type=MESH,
            )
        )
        copies[-1].start()
    own.wait()
    for copy in copies:
        copy.wait()
    copies = []
    for index, peer in enumerate(col_peers):
        copies.append(
            pltpu.make_async_remote_copy(
                src_ref=all_ref.at[col],
                dst_ref=all_ref.at[col],
                send_sem=send_sems.at[n_rows + index],
                recv_sem=recv_sems.at[n_rows + index],
                device_id={"cols": peer},
                device_id_type=MESH,
            )
        )
        copies[-1].start()
    for copy in copies:
        copy.wait()


def mark(tile_cols, tile_counts, n_rows, n_cols, size):
    steps = tile_cols.shape[0]
    return pl.pallas_call(
        functools.partial(mark_kernel, n_rows, n_cols, steps),
        out_shape=jax.ShapeDtypeStruct((n_cols, n_rows, steps * n_rows, size), jnp.bfloat16),
        in_specs=[VM, SM],
        out_specs=VM,
        scratch_shapes=[
            pltpu.VMEM((steps * n_rows, size), jnp.bfloat16),
            pltpu.SemaphoreType.DMA((n_rows + n_cols,)),
            pltpu.SemaphoreType.DMA((n_rows + n_cols,)),
            pltpu.SemaphoreType.DMA,
        ],
        compiler_params=pltpu.CompilerParams(collective_id=0, has_side_effects=True),
        name="mark",
    )(tile_cols, tile_counts)


def plan_kernel(
    n_rows, steps, all_ref, cols_ref, count_ref, code_ref, list_ref, tier_ref, keys, shared_keys, table
):
    team, row, half, _, _, _ = teams(n_rows)
    col = lax.axis_index("cols")
    size = all_ref.shape[-1]
    n_cols = all_ref.shape[0]
    depth = steps * n_rows
    before = lax.broadcasted_iota(jnp.int32, (size, size), 0)
    after = lax.broadcasted_iota(jnp.int32, (size, size), 1)
    triangle = jnp.where(before < after, 1.0, 0.0).astype(jnp.bfloat16)

    def ranks(flags):
        flat = flags.reshape(-1, size).astype(jnp.bfloat16)
        return jnp.dot(flat, triangle, preferred_element_type=jnp.float32).reshape(flags.shape)

    owner = lax.rem(lax.broadcasted_iota(jnp.int32, (1, depth, size), 1), n_rows)
    most_listed, most_shared = [], []
    for part in range(2):
        needs = all_ref[:, part * team : (part + 1) * team].astype(jnp.float32)
        near = owner // team == part
        wanted = needs[:, 0]
        for index in range(1, team):
            wanted = wanted + needs[:, index]
        alone = near | (wanted < 1.5)
        listed = jnp.where(alone[:, None], needs, 0.0)
        rank = ranks(listed)
        over = jnp.where(rank >= SPILL, listed, 0.0)
        spilled = over[:, 0]
        for index in range(1, team):
            spilled = jnp.maximum(spilled, over[:, index])
        shared = jnp.where(near | ((wanted < 1.5) & (spilled < 0.5)), 0.0, 1.0)
        shared_rank = ranks(shared)
        keep = (listed > 0.5) & (near[:, None] | (rank < SPILL))
        keys[:, part * team : (part + 1) * team] = jnp.where(keep, rank, -1.0)
        shared_keys[:, part] = jnp.where(shared > 0.5, shared_rank, -1.0)
        most_listed.append(jnp.max(jnp.where(keep & near[:, None], rank, -1.0)))
        most_shared.append(jnp.max(jnp.where(shared > 0.5, shared_rank, -1.0)))
    listed = jnp.maximum(*most_listed) + 1.0
    shared = jnp.maximum(*most_shared) + 1.0
    tier = jnp.int32(0)
    for cap, shared_cap in TIERS:
        tier = tier + jnp.where((listed > cap) | (shared > shared_cap), 1, 0).astype(jnp.int32)
    tier_ref[0] = tier

    table[...] = jnp.full_like(table, -1.0)
    sub = lax.broadcasted_iota(jnp.int32, (n_rows, size), 0)
    slot = lax.rem(sub, team)
    n_lists = 2 * team + 1
    for s in range(steps):
        mine = pl.ds(s * n_rows + row, 1)
        for index in range(team):
            at = 2 * n_rows * s + index
            table[at : at + 1, :] = keys[col, half * team + index, mine, :]
            table[at + team : at + team + 1, :] = keys[col, (1 - half) * team + index, mine, :]
        at = 2 * n_rows * s + 2 * team
        table[at : at + 1, :] = shared_keys[col, 1 - half, mine, :]
        block = pl.ds(s * n_rows, n_rows)
        listed_key = keys[col, row, block, :]
        shared_key = shared_keys[col, half, block, :]
        kind = jnp.where(sub // team == half, slot, team + slot)
        value = (kind * size).astype(jnp.float32) + listed_key
        other = ((2 * team + slot) * size).astype(jnp.float32) + shared_key
        at = 2 * n_rows * steps + s * n_rows
        table[at : at + n_rows, :] = jnp.where(shared_key >= 0.0, other, value)
    flipped = table[...].T
    lane = after.astype(jnp.float32)
    down = before.astype(jnp.float32)
    for s in range(steps):
        for index in range(n_lists):
            at = 2 * n_rows * s + index
            hit = flipped[:, at : at + 1] == lane
            picked = jnp.sum(jnp.where(hit, down, 0.0), axis=0, keepdims=True)
            list_ref[s : s + 1, index * size : (index + 1) * size] = picked.astype(jnp.int32)
    for s, (cols, live) in enumerate(slots_of(cols_ref[...], lambda s: count_ref[s, 0, 0], steps)):
        chosen = jnp.zeros((size, size), jnp.float32)
        for index in range(n_rows):
            at = 2 * n_rows * steps + s * n_rows + index
            chosen = jnp.where(cols >> 7 == index, flipped[:, at : at + 1], chosen)
        code = jnp.sum(jnp.where((cols & 127) == before, chosen, 0.0), axis=0, keepdims=True)
        code_ref[s : s + 1, :] = jnp.where(live, code, 0.0).astype(jnp.int32)


def plan(everyone, tile_cols, tile_counts, n_rows):
    steps, slots = tile_cols.shape
    size = everyone.shape[-1]
    lists = n_rows + 1
    return pl.pallas_call(
        functools.partial(plan_kernel, n_rows, steps),
        out_shape=(
            jax.ShapeDtypeStruct((steps, slots), jnp.int32),
            jax.ShapeDtypeStruct((steps, lists * size), jnp.int32),
            jax.ShapeDtypeStruct((1,), jnp.int32),
        ),
        in_specs=[VM, VM, SM],
        out_specs=(VM, VM, SM),
        scratch_shapes=[
            pltpu.VMEM(everyone.shape, jnp.float32),
            pltpu.VMEM((everyone.shape[0], 2, *everyone.shape[2:]), jnp.float32),
            pltpu.VMEM((size, size), jnp.float32),
        ],
        compiler_params=LOCAL,
        name="plan",
    )(everyone, tile_cols, tile_counts)


class Room:
    def __init__(self, team, listed, shared):
        self.team, self.listed, self.shared = team, listed, shared
        self.spill = team * listed
        self.common = self.spill + team * SPILL
        self.packed = self.common + shared
        self.spread = self.common + team * shared

    def near(self, index):
        return pl.ds(index * self.listed, self.listed)

    def far(self, index):
        return pl.ds(self.spill + index * SPILL, SPILL)

    def group(self, index):
        return pl.ds(self.common + index * self.shared, self.shared)

    def place(self, code, size):
        kind, rank = code // size, lax.rem(code, size)
        far = self.spill + (kind - self.team) * SPILL
        common = self.common + (kind - 2 * self.team) * self.shared
        base = jnp.where(kind < 2 * self.team, far, common)
        return jnp.where(kind < self.team, kind * self.listed, base) + rank

    def entries(self, body):
        def run(first, lists, count, start):
            @pl.loop(0, count)
            def _(index):
                for which in range(lists):
                    body(start + which * count + index, first + which, index)

        run(0, self.team, self.listed, 0)
        run(self.team, self.team, SPILL, self.spill)
        run(2 * self.team, 1, self.shared, self.common)


def pack_lists(room, step, lists_ref, weights_ref, send_ref):
    size = send_ref.shape[-1]

    def body(entry, which, index):
        where = lanes(lists_ref[step, which * size + index], size)
        send_ref[entry] = weights_ref[:, where].astype(jnp.bfloat16)

    room.entries(body)


def apply_lists(room, step, lists_ref, rate_ref, weights_ref, grads_ref, out_ref):
    size = grads_ref.shape[-1]
    out_ref[...] = weights_ref[...]
    rate = rate_ref[step]

    def body(entry, which, index):
        where = lanes(lists_ref[step, which * size + index], size)
        out_ref[:, where] -= rate * grads_ref[entry].astype(jnp.float32)

    room.entries(body)


def apply_pack_lists(room, step, lists_ref, rate_ref, weights_ref, grads_ref, out_ref, send_ref):
    apply_lists(room, step, lists_ref, rate_ref, weights_ref, grads_ref, out_ref)
    pack_lists(room, step + 1, lists_ref, out_ref, send_ref)


def row_copy(sems, index, src, dst, peer):
    return pltpu.make_async_remote_copy(
        src_ref=src,
        dst_ref=dst,
        send_sem=sems[0].at[index],
        recv_sem=sems[1].at[index],
        device_id={"rows": peer},
        device_id_type=MESH,
    )


def spread_kernel(room, n_rows, send_ref, got_ref, send_sems, recv_sems, own_sem):
    team, _, _, place, mate, other = teams(n_rows)
    sems = (send_sems, recv_sems)
    shifts = range(1, team)
    entered = greet_rows([mate(s) for s in shifts] + [other(s) for s in range(team)])
    own = pltpu.make_async_copy(send_ref.at[room.near(place)], got_ref.at[room.near(place)], own_sem)
    own.start()
    entered()
    common = pl.ds(room.common, room.shared)
    group = row_copy(sems, 0, send_ref.at[common], got_ref.at[room.group(place)], other(0))
    group.start()
    copies = []
    for shift in range(team):
        to = lax.rem(place + shift, team)
        copies.append(row_copy(
            sems, 1 + shift, send_ref.at[room.far(to)], got_ref.at[room.far(place)], other(shift)
        ))
        copies[-1].start()
    for shift in shifts:
        to = lax.rem(place + shift, team)
        copies.append(row_copy(
            sems, team + shift, send_ref.at[room.near(to)], got_ref.at[room.near(place)], mate(shift)
        ))
        copies[-1].start()
    group.wait_recv()
    for shift in shifts:
        mine = room.group(place)
        copies.append(row_copy(
            sems, 2 * team - 1 + shift, got_ref.at[mine], got_ref.at[mine], mate(shift)
        ))
        copies[-1].start()
    group.wait_send()
    own.wait()
    for copy in copies:
        copy.wait()


def gather_kernel(room, n_rows, grads_ref, out_ref, pool, total, send_sems, recv_sems, own_sem):
    team, _, _, place, mate, other = teams(n_rows)
    sems = (send_sems, recv_sems)
    shifts = range(1, team)
    entered = greet_rows([mate(s) for s in shifts] + [other(s) for s in range(team)])
    own = pltpu.make_async_copy(grads_ref.at[room.near(place)], out_ref.at[room.near(place)], own_sem)
    own.start()
    entered()
    pools, copies = [], []
    for shift in shifts:
        to = lax.rem(place + shift, team)
        pools.append(row_copy(
            sems, shift, grads_ref.at[room.group(to)], pool.at[shift - 1], mate(shift)
        ))
        pools[-1].start()
    for shift in range(team):
        to = lax.rem(place + shift, team)
        copies.append(row_copy(
            sems, team + shift, grads_ref.at[room.far(to)], out_ref.at[room.far(place)], other(shift)
        ))
        copies[-1].start()
    for shift in shifts:
        to = lax.rem(place + shift, team)
        copies.append(row_copy(
            sems, 2 * team - 1 + shift, grads_ref.at[room.near(to)], out_ref.at[room.near(place)],
            mate(shift),
        ))
        copies[-1].start()
    for copy in pools:
        copy.wait_recv()

    mine = room.common + place * room.shared

    @pl.loop(0, room.shared)
    def _(index):
        value = grads_ref[mine + index].astype(jnp.float32)
        for part in range(team - 1):
            value = value + pool[part, index].astype(jnp.float32)
        total[index] = value.astype(jnp.bfloat16)

    common = pl.ds(room.common, room.shared)
    group = row_copy(sems, 0, total, out_ref.at[common], other(0))
    group.start()
    for copy in pools:
        copy.wait_send()
    own.wait()
    for copy in copies:
        copy.wait()
    group.wait()


def remote_sems(count):
    return [pltpu.SemaphoreType.DMA((count,)), pltpu.SemaphoreType.DMA((count,)), pltpu.SemaphoreType.DMA]


def team_program(
    n_rows, listed, shared, branch, code, lists,
    tiles, tile_scales, tile_rows, tile_cols, tile_counts, labels, learning_rate, weights
):
    classes = weights.shape[0]
    size = tiles.shape[-1]
    steps, slots = tiles.shape[0], tiles.shape[3]
    n_cols = lax.axis_size("cols")
    samples = labels.shape[1]
    owned = samples // n_cols
    room = Room(n_rows // 2, listed, shared)
    packed = jax.ShapeDtypeStruct((room.packed, classes, size), jnp.bfloat16)
    spread = jax.ShapeDtypeStruct((room.spread, classes, size), jnp.bfloat16)
    scalars = (code, tile_rows, tile_scales, tile_counts)
    in_hbm = pl.BlockSpec(memory_space=pltpu.HBM)
    tile_room = [pltpu.VMEM(tiles.shape[3:], tiles.dtype), pltpu.SemaphoreType.DMA((slots // GROUP,))]

    def remote(index):
        return pltpu.CompilerParams(
            collective_id=1 + steps + 2 * branch + index, has_side_effects=True,
            vmem_limit_bytes=VMEM_LIMIT,
        )

    current = weights
    send = pl.pallas_call(
        functools.partial(pack_lists, room, 0),
        out_shape=packed, in_specs=[SM, VM], out_specs=VM, compiler_params=LOCAL, name="pack",
    )(lists, current)
    losses = []
    for step in range(steps):
        got = pl.pallas_call(
            functools.partial(spread_kernel, room, n_rows),
            out_shape=spread, in_specs=[VM], out_specs=VM, compiler_params=remote(0),
            scratch_shapes=remote_sems(3 * room.team - 1), name="spread",
        )(send)
        part = pl.pallas_call(
            functools.partial(scores_kernel, step, lambda x: room.place(x, size)),
            out_shape=jax.ShapeDtypeStruct((classes, samples), jnp.float32),
            in_specs=[SM] * 4 + [VM, in_hbm], out_specs=VM, compiler_params=SLOTS,
            scratch_shapes=tile_room, name="scores",
        )(*scalars, got, tiles)
        residual, loss = classify(step, n_cols, part, labels)
        losses.append(loss)
        grads = pl.pallas_call(
            functools.partial(grads_kernel, step, lambda x: room.place(x, size)),
            out_shape=spread,
            in_specs=[SM] * 4 + [VM, in_hbm], out_specs=VM, compiler_params=SLOTS,
            scratch_shapes=[pltpu.VMEM((room.spread, classes, size), jnp.float32), *tile_room],
            name="grads",
        )(*scalars, residual, tiles)
        grads = pl.pallas_call(
            functools.partial(gather_kernel, room, n_rows),
            out_shape=packed, in_specs=[VM], out_specs=VM, compiler_params=remote(1),
            scratch_shapes=[
                pltpu.VMEM((room.team - 1, shared, classes, size), jnp.bfloat16),
                pltpu.VMEM((shared, classes, size), jnp.bfloat16),
                *remote_sems(3 * room.team - 1),
            ],
            name="gather",
        )(grads)
        shape = jax.ShapeDtypeStruct(current.shape, current.dtype)
        more = step + 1 < steps
        current, *send = pl.pallas_call(
            functools.partial(apply_pack_lists if more else apply_lists, room, step),
            out_shape=(shape, packed) if more else (shape,),
            in_specs=[SM, SM, VM, VM], out_specs=(VM, VM) if more else (VM,),
            compiler_params=LOCAL, name="apply",
        )(lists, learning_rate, current, grads)
        send = send[0] if more else None
    return current, jnp.concatenate(losses)


def team_device(
    tiles, tile_scales, tile_rows, tile_cols, tile_counts, labels, learning_rate, weights
):
    args = (tiles, tile_scales, tile_rows, tile_cols, tile_counts, labels, learning_rate, weights)
    size = tiles.shape[-1]
    n_rows, n_cols = lax.axis_size("rows"), lax.axis_size("cols")
    cols = tile_cols[:, 0, 0]
    everyone = mark(cols, tile_counts, n_rows, n_cols, size)
    code, lists, tier = plan(everyone, cols, tile_counts, n_rows)
    branches = [
        functools.partial(team_program, n_rows, listed, shared, branch)
        for branch, (listed, shared) in enumerate((*TIERS, (size, size)))
    ]
    return lax.switch(tier[0], branches, code, lists, *args)


def either_device(*args):
    tiles, weights, labels = args[0], args[-1], args[5]
    n_rows, n_cols = lax.axis_size("rows"), lax.axis_size("cols")
    size, steps = tiles.shape[-1], tiles.shape[0]
    even = n_rows == 8 and steps * n_rows * 3 <= size and labels.shape[1] // n_cols % size == 0
    if even and size == 128 and weights.shape[1] == size * size:
        return team_device(*args)
    return per_device(*args)


def solution(mesh):
    return jax.shard_map(
        either_device,
        mesh=mesh,
        in_specs=(
            P(None, "rows", "cols", None, None, None),
            P(None, "rows", "cols", None),
            P(None, "rows", "cols", None),
            P(None, "rows", "cols", None),
            P(None, "rows", "cols"),
            P(None, "rows"),
            P(),
            P(None, ("cols", "rows")),
        ),
        out_specs=(P(None, ("cols", "rows")), P(None, ("rows", "cols"))),
        check_vma=False,
    )
```

profile of v0, /device:TPU:0, one launch (start us, length us, event | category | flops | bytes accessed | tf_op | source)
XLA Modules:
  0.0 190.2 jit_solution(17497830096567979843)
XLA Ops:
  0.6 1.3 copy.20.count_ref
  1.9 13.5 %mark.1.all_ref = bf16[4,8,16,128]{3,2,1,0:T(8,128)(2,1)} custom-call(s32[2,128]{1,0:T(2,128)} %bitcast.2, s32[2,1,1]{2,1,0:T(1,128)} %copy.20.count_ref), custom_call_target="tpu_custom_call" | custom-call | tf_op jit(solution)/shard_map/mark/pallas_call | solution.py:498
  15.4 0.9 copy-done.13
  16.3 0.7 copy-done.24
  17.0 0.7 copy-done.25
  17.7 2.0 %plan.1 = (s32[2,128]{1,0:T(2,128)S(1)}, s32[2,1152]{1,0:T(2,128)S(1)}, s32[1]{0:T(128)}) custom-call(bf16[4,8,16,128]{3,2,1,0:T(8,128)(2,1)S(1)} %copy-done.13, s32[2,128]{1,0:T(2,128)S(1)} %bitcast.3, s32[2,1,1]{2,1,0:T(1,128)S(1)} %copy-done.25), custom_call_target="tpu_custom_call" | custom-call | tf_op jit(solution)/shard_map/plan/pallas_call | solution.py:601
  20.4 169.8 %conditional.1 = (f32[32,16384]{1,0:T(8,128)}, f32[2,256]{1,0:T(2,128)}) conditional(s32[]{:T(128)} %bitcast.1, (s32[2,1152]{1,0:T(2,128)S(1)}, f32[32,16384]{1,0:T(8,128)}, s32[2,128]{1,0:T(2,128)S(1)}, s32[2,1,1,128]{3,2,1,0:T(1,128)}, f32[2,1,1,128]{3,2,1,0:T(1,128)}, /*index=5*/s32[2,1,1]{0,2,1:T(1,128)}, ...), branch_computations={%region_0.0_spmd, %region_1.0_spmd, %region_2.0_spmd, %region_3.0_... | conditional | flops 512 | bytes 77644200 | solution.py:871
  20.4 0.7 copy.23.count_ref
  21.1 2.4 %pack.6.send_ref = bf16[160,32,128]{2,1,0:T(8,128)(2,1)S(1)} custom-call(s32[2,1152]{1,0:T(2,128)S(1)} %get-tuple-element.105.lists_ref, f32[32,16384]{1,0:T(8,128)} %get-tuple-element.107.weights_ref), custom_call_target="tpu_custom_call" | custom-call | tf_op jit(solution)/shard_map/cond/branch_1_fun/pack/pallas_call | solution.py:810
  23.6 30.1 %spread.12.recv_ref = bf16[208,32,128]{2,1,0:T(8,128)(2,1)S(1)} custom-call(bf16[160,32,128]{2,1,0:T(8,128)(2,1)S(1)} %pack.6.send_ref), custom_call_target="tpu_custom_call" | custom-call | tf_op jit(solution)/shard_map/cond/branch_1_fun/spread/pallas_call | solution.py:816
  53.7 4.9 %scores.12.part_ref = f32[32,1024]{1,0:T(8,128)S(1)} custom-call(s32[2,128]{1,0:T(2,128)S(1)} %get-tuple-element.108.code_ref, s32[2,1,1,128]{3,2,1,0:T(1,128)S(1)} %copy-done.36, f32[2,1,1,128]{3,2,1,0:T(1,128)S(1)} %copy-done.41, s32[2,1,1]{2,1,0:T(1,128)S(1)} %copy.23.count_ref, bf16[208,32,128]{2,1,0:T(8,128)(2,1)S(1)} %spread.12.recv_ref, ...), custom_call_target="tpu_custom_call" | custom-call | tf_op jit(solution)/shard_map/cond/branch_1_fun/scores/pallas_call | solution.py:821
  59.3 8.3 %classify.12 = (bf16[32,1024]{1,0:T(8,128)(2,1)}, f32[1,256]{1,0:T(1,128)}) custom-call(f32[32,1024]{1,0:T(8,128)} %copy-done.5, s32[2,1024]{1,0:T(2,128)S(1)} %copy-done.31), custom_call_target="tpu_custom_call" | custom-call | tf_op jit(solution)/shard_map/cond/branch_1_fun/classify/pallas_call | solution.py:255
  67.6 0.8 copy-done.20
  68.5 4.1 %grads.12.grads_ref = bf16[208,32,128]{2,1,0:T(8,128)(2,1)S(1)} custom-call(s32[2,128]{1,0:T(2,128)S(1)} %get-tuple-element.108.code_ref, s32[2,1,1,128]{3,2,1,0:T(1,128)S(1)} %copy-done.36, f32[2,1,1,128]{3,2,1,0:T(1,128)S(1)} %copy-done.41, s32[2,1,1]{2,1,0:T(1,128)S(1)} %copy.23.count_ref, bf16[32,1024]{1,0:T(8,128)(2,1)S(1)} %copy-done.20, ...), custom_call_target="tpu_custom_call" | custom-call | tf_op jit(solution)/shard_map/cond/branch_1_fun/grads/pallas_call | solution.py:829
  72.6 29.3 %gather.12.grads_ref = bf16[160,32,128]{2,1,0:T(8,128)(2,1)S(1)} custom-call(bf16[208,32,128]{2,1,0:T(8,128)(2,1)S(1)} %grads.12.grads_ref), custom_call_target="tpu_custom_call" | custom-call | tf_op jit(solution)/shard_map/cond/branch_1_fun/gather/pallas_call | solution.py:836
  101.9 2.9 %apply.12 = (f32[32,16384]{1,0:T(8,128)S(1)}, bf16[160,32,128]{2,1,0:T(8,128)(2,1)S(1)}) custom-call(s32[2,1152]{1,0:T(2,128)S(1)} %get-tuple-element.105.lists_ref, f32[2]{0:T(128)S(1)} %copy-done.46, f32[32,16384]{1,0:T(8,128)S(1)} %copy-done.27, bf16[160,32,128]{2,1,0:T(8,128)(2,1)S(1)} %gather.12.grads_ref), custom_call_target="tpu_custom_call" | custom-call | tf_op jit(solution)/shard_map/cond/branch_1_fun/apply/pallas_call | solution.py:848
  104.8 30.8 %spread.13.recv_ref = bf16[208,32,128]{2,1,0:T(8,128)(2,1)S(1)} custom-call(bf16[160,32,128]{2,1,0:T(8,128)(2,1)S(1)} %get-tuple-element.116.send_ref), custom_call_target="tpu_custom_call" | custom-call | tf_op jit(solution)/shard_map/cond/branch_1_fun/spread/pallas_call | solution.py:816
  135.5 4.9 %scores.13.part_ref = f32[32,1024]{1,0:T(8,128)S(1)} custom-call(s32[2,128]{1,0:T(2,128)S(1)} %get-tuple-element.108.code_ref, s32[2,1,1,128]{3,2,1,0:T(1,128)S(1)} %copy-done.36, f32[2,1,1,128]{3,2,1,0:T(1,128)S(1)} %copy-done.41, s32[2,1,1]{2,1,0:T(1,128)S(1)} %copy.23.count_ref, bf16[208,32,128]{2,1,0:T(8,128)(2,1)S(1)} %spread.13.recv_ref, ...), custom_call_target="tpu_custom_call" | custom-call | tf_op jit(solution)/shard_map/cond/branch_1_fun/scores/pallas_call | solution.py:821
  141.1 9.5 %classify.13 = (bf16[32,1024]{1,0:T(8,128)(2,1)}, f32[1,256]{1,0:T(1,128)}) custom-call(f32[32,1024]{1,0:T(8,128)} %copy-done.6, s32[2,1024]{1,0:T(2,128)S(1)} %copy-done.31), custom_call_target="tpu_custom_call" | custom-call | tf_op jit(solution)/shard_map/cond/branch_1_fun/classify/pallas_call | solution.py:255
  150.7 1.2 pad_maximum_fusion.1
  151.9 0.8 copy-done.15
  152.7 4.1 %grads.13.grads_ref = bf16[208,32,128]{2,1,0:T(8,128)(2,1)S(1)} custom-call(s32[2,128]{1,0:T(2,128)S(1)} %get-tuple-element.108.code_ref, s32[2,1,1,128]{3,2,1,0:T(1,128)S(1)} %copy-done.36, f32[2,1,1,128]{3,2,1,0:T(1,128)S(1)} %copy-done.41, s32[2,1,1]{2,1,0:T(1,128)S(1)} %copy.23.count_ref, bf16[32,1024]{1,0:T(8,128)(2,1)S(1)} %copy-done.15, ...), custom_call_target="tpu_custom_call" | custom-call | tf_op jit(solution)/shard_map/cond/branch_1_fun/grads/pallas_call | solution.py:829
  156.8 30.0 %gather.13.grads_ref = bf16[160,32,128]{2,1,0:T(8,128)(2,1)S(1)} custom-call(bf16[208,32,128]{2,1,0:T(8,128)(2,1)S(1)} %grads.13.grads_ref), custom_call_target="tpu_custom_call" | custom-call | tf_op jit(solution)/shard_map/cond/branch_1_fun/gather/pallas_call | solution.py:836
  186.8 3.3 %apply.13 = f32[32,16384]{1,0:T(8,128)} custom-call(s32[2,1152]{1,0:T(2,128)S(1)} %get-tuple-element.105.lists_ref, f32[2]{0:T(128)S(1)} %copy-done.46, f32[32,16384]{1,0:T(8,128)S(1)} %get-tuple-element.115.weights_ref, bf16[160,32,128]{2,1,0:T(8,128)(2,1)S(1)} %gather.13.grads_ref), custom_call_target="tpu_custom_call" | custom-call | tf_op jit(solution)/shard_map/cond/branch_1_fun/apply/pallas_call | solution.py:848
  (21 shorter events, 1.3 us)
Async XLA Ops:
  15.4 0.9 copy-start.13
  16.3 0.7 copy-start.24
  17.0 0.7 copy-start.25
  23.6 30.1 %copy-start.36 = (s32[2,1,1,128]{3,2,1,0:T(1,128)S(1)}, s32[2,1,1,128]{3,2,1,0:T(1,128)}, u32[]{:S(2)}) copy-start(s32[2,1,1,128]{3,2,1,0:T(1,128)} %get-tuple-element.109.row_ref) | copy-start | bytes 3076 | tf_op jit(solution)/shard_map/cond
  23.6 30.1 %copy-start.41 = (f32[2,1,1,128]{3,2,1,0:T(1,128)S(1)}, f32[2,1,1,128]{3,2,1,0:T(1,128)}, u32[]{:S(2)}) copy-start(f32[2,1,1,128]{3,2,1,0:T(1,128)} %get-tuple-element.110.scale_ref) | copy-start | bytes 3076 | tf_op jit(solution)/shard_map/cond
  53.7 5.6 %copy-start.31 = (s32[2,1024]{1,0:T(2,128)S(1)}, s32[2,1024]{1,0:T(2,128)}, u32[]{:S(2)}) copy-start(s32[2,1024]{1,0:T(2,128)} %get-tuple-element.113.labels_ref) | copy-start | bytes 24580 | tf_op jit(solution)/shard_map/cond
  58.6 0.7 copy-start.5
  67.6 0.8 copy-start.20
  72.5 29.3 %copy-start.27 = (f32[32,16384]{1,0:T(8,128)S(1)}, f32[32,16384]{1,0:T(8,128)}, u32[]{:S(2)}) copy-start(f32[32,16384]{1,0:T(8,128)} %get-tuple-element.107.weights_ref) | copy-start | bytes 6291460 | tf_op jit(solution)/shard_map/cond
  72.5 29.3 %copy-start.46 = (f32[2]{0:T(128)S(1)}, f32[2]{0:T(128)}, u32[]{:S(2)}) copy-start(f32[2]{0:T(128)} %get-tuple-element.106.rate_ref) | copy-start | bytes 28 | tf_op jit(solution)/shard_map/cond
  135.5 15.1 %copy-start.51 = (f32[1,256]{1,0:T(1,128)S(1)}, f32[1,256]{1,0:T(1,128)}, u32[]{:S(2)}) copy-start(f32[1,256]{1,0:T(1,128)} %get-tuple-element.118) | copy-start | bytes 3076 | tf_op jit(solution)/shard_map/cond
  140.4 0.7 copy-start.6
  151.9 0.8 copy-start.15
where the time goes:
time: 191 us; the launch traced here: 190 us
  Pallas kernels  180 us (94%)
  local copies, waits for them, and re-layouts  7.3 us (4%)
    pallas_call x2, Pallas kernels, team_program(): pl.pallas_call(functools.partial(spread_kernel, room, n_rows), out_shape=...  60.9 us
    pallas_call x2, Pallas kernels, team_program(): pl.pallas_call(functools.partial(gather_kernel, room, n_rows), out_shape=...  59.3 us
    pallas_call x2, Pallas kernels, classify(): pl.pallas_call(functools.partial(classify_kernel, 'cols', n_cols, step),...  17.9 us
    pallas_call x1, Pallas kernels, mark(): pl.pallas_call(functools.partial(mark_kernel, n_rows, n_cols, steps), out...  13.5 us
    pallas_call x2, Pallas kernels, team_program(): pl.pallas_call(functools.partial(scores_kernel, step, lambda x: room.plac...  9.78 us
    pallas_call x2, Pallas kernels, team_program(): pl.pallas_call(functools.partial(grads_kernel, step, lambda x: room.place...  8.13 us
    pallas_call x2, Pallas kernels, team_program(): pl.pallas_call(functools.partial(apply_pack_lists if more else apply_list...  6.21 us

commit v1 on v0

--- a/solution.py
+++ b/solution.py
@@ -422,6 +422,11 @@
     mate = lambda shift: half * team + lax.rem(place + shift, team)
     other = lambda shift: (1 - half) * team + lax.rem(place + shift, team)
     return team, row, half, place, mate, other
+
+
+def corners(place):
+    beside = place + 1 - 2 * lax.rem(place, 2)
+    return beside, lax.rem(place + 2, 4), lax.rem(beside + 2, 4)
 
 
 def greet_rows(peers):
@@ -617,6 +622,74 @@
     )(everyone, tile_cols, tile_counts)
 
 
+def split_classify_kernel(
+    count, step, part_ref, labels_ref, residual_ref, loss_ref, held, send_sems, recv_sems
+):
+    me = lax.axis_index("cols")
+    owned = loss_ref.shape[1]
+    barrier = pltpu.get_barrier_semaphore()
+    peers = [lax.rem(me + shift, count) for shift in range(1, count)]
+    for peer in peers:
+        pl.semaphore_signal(barrier, inc=1, device_id={"cols": peer}, device_id_type=MESH)
+    mine = lanes(me, owned)
+
+    def copy(index, src, dst, peer):
+        return pltpu.make_async_remote_copy(
+            src_ref=src,
+            dst_ref=dst,
+            send_sem=send_sems.at[index],
+            recv_sem=recv_sems.at[index],
+            device_id={"cols": peer},
+            device_id_type=MESH,
+        )
+
+    pl.semaphore_wait(barrier, count - 1)
+    parts = [copy(i, part_ref.at[:, lanes(peer, owned)], held.at[i], peer) for i, peer in enumerate(peers)]
+    for part in parts:
+        part.start()
+    class_ids = lax.broadcasted_iota(jnp.int32, held.shape[1:], 0)
+    onehot = (class_ids == labels_ref[step : step + 1, mine]).astype(jnp.float32)
+    scores = part_ref[:, mine]
+    for index, part in enumerate(parts):
+        part.wait_recv()
+        scores = scores + held[index]
+    exp_scores = jnp.exp(scores)
+    total = jnp.sum(exp_scores, axis=0, keepdims=True)
+    residual_ref[:, mine] = (exp_scores / total - onehot).astype(jnp.bfloat16)
+    loss_ref[...] = jnp.log(total) - jnp.sum(onehot * scores, axis=0, keepdims=True)
+    shared = residual_ref.at[:, mine]
+    sent = [copy(count + i, shared, shared, peer) for i, peer in enumerate(peers)]
+    for part in sent:
+        part.start()
+    for part in parts:
+        part.wait_send()
+    for part in sent:
+        part.wait()
+
+
+def split_classify(step, n_cols, part, labels):
+    classes, samples = part.shape
+    owned = samples // n_cols
+    return pl.pallas_call(
+        functools.partial(split_classify_kernel, n_cols, step),
+        out_shape=(
+            jax.ShapeDtypeStruct((classes, samples), jnp.bfloat16),
+            jax.ShapeDtypeStruct((1, owned), jnp.float32),
+        ),
+        in_specs=[VM, VM],
+        out_specs=(VM, VM),
+        scratch_shapes=[
+            pltpu.VMEM((n_cols - 1, classes, owned), jnp.float32),
+            pltpu.SemaphoreType.DMA((2 * n_cols,)),
+            pltpu.SemaphoreType.DMA((2 * n_cols,)),
+        ],
+        compiler_params=pltpu.CompilerParams(
+            collective_id=1 + step, has_side_effects=True, vmem_limit_bytes=VMEM_LIMIT
+        ),
+        name="classify",
+    )(part, labels)
+
+
 class Room:
     def __init__(self, team, listed, shared):
         self.team, self.listed, self.shared = team, listed, shared
@@ -691,87 +764,99 @@
     )
 
 
-def spread_kernel(room, n_rows, send_ref, got_ref, send_sems, recv_sems, own_sem):
-    team, _, _, place, mate, other = teams(n_rows)
+def spread_kernel(room, n_rows, send, got_ref, send_sems, recv_sems, own_sem):
+    team, _, half, place, _, other = teams(n_rows)
     sems = (send_sems, recv_sems)
-    shifts = range(1, team)
-    entered = greet_rows([mate(s) for s in shifts] + [other(s) for s in range(team)])
-    own = pltpu.make_async_copy(send_ref.at[room.near(place)], got_ref.at[room.near(place)], own_sem)
+    beside, across, corner = corners(place)
+    entered = greet_rows([half * team + to for to in (beside, across, corner)] + [other(s) for s in range(team)])
+
+    def to_mate(index, src, dst, mate):
+        copies.append(row_copy(sems, index, src, got_ref.at[dst], half * team + mate))
+        copies[-1].start()
+        return copies[-1]
+
+    copies = []
+    common = pl.ds(room.common, room.shared)
+    own = pltpu.make_async_copy(send.at[room.near(place)], got_ref.at[room.near(place)], own_sem)
     own.start()
     entered()
-    common = pl.ds(room.common, room.shared)
-    group = row_copy(sems, 0, send_ref.at[common], got_ref.at[room.group(place)], other(0))
+    group = row_copy(sems, 0, send.at[common], got_ref.at[room.group(place)], other(0))
     group.start()
-    copies = []
     for shift in range(team):
         to = lax.rem(place + shift, team)
         copies.append(row_copy(
-            sems, 1 + shift, send_ref.at[room.far(to)], got_ref.at[room.far(place)], other(shift)
+            sems, 1 + shift, send.at[room.far(to)], got_ref.at[room.far(place)], other(shift)
         ))
         copies[-1].start()
-    for shift in shifts:
-        to = lax.rem(place + shift, team)
-        copies.append(row_copy(
-            sems, team + shift, send_ref.at[room.near(to)], got_ref.at[room.near(place)], mate(shift)
-        ))
-        copies[-1].start()
+    to_mate(8, send.at[room.near(beside)], room.near(place), beside)
     group.wait_recv()
-    for shift in shifts:
-        mine = room.group(place)
-        copies.append(row_copy(
-            sems, 2 * team - 1 + shift, got_ref.at[mine], got_ref.at[mine], mate(shift)
-        ))
-        copies[-1].start()
+    mine = room.group(place)
+    passed = to_mate(6, got_ref.at[mine], mine, across)
+    to_mate(5, got_ref.at[mine], mine, beside)
+    to_mate(9, send.at[room.near(across)], room.near(place), across)
+    to_mate(10, send.at[room.near(corner)], room.near(place), corner)
+
+    passed.wait_recv()
+    theirs = room.group(across)
+    to_mate(7, got_ref.at[theirs], theirs, beside)
+    passed.wait_send()
     group.wait_send()
     own.wait()
     for copy in copies:
-        copy.wait()
-
-
-def gather_kernel(room, n_rows, grads_ref, out_ref, pool, total, send_sems, recv_sems, own_sem):
-    team, _, _, place, mate, other = teams(n_rows)
+        if copy is not passed:
+            copy.wait()
+
+
+def gather_kernel(
+    room, n_rows, grads_ref, out_ref, pool, passing, total, send_sems, recv_sems, own_sem
+):
+    team, _, half, place, _, other = teams(n_rows)
     sems = (send_sems, recv_sems)
-    shifts = range(1, team)
-    entered = greet_rows([mate(s) for s in shifts] + [other(s) for s in range(team)])
+    beside, across, corner = corners(place)
+    entered = greet_rows([half * team + to for to in (beside, across, corner)] + [other(s) for s in range(team)])
     own = pltpu.make_async_copy(grads_ref.at[room.near(place)], out_ref.at[room.near(place)], own_sem)
     own.start()
     entered()
-    pools, copies = [], []
-    for shift in shifts:
-        to = lax.rem(place + shift, team)
-        pools.append(row_copy(
-            sems, shift, grads_ref.at[room.group(to)], pool.at[shift - 1], mate(shift)
-        ))
-        pools[-1].start()
+
+    def to_mate(index, src, dst, mate):
+        copy = row_copy(sems, index, src, dst, half * team + mate)
+        copy.start()
+        return copy
+
+    def near(index, to):
+        copies.append(to_mate(index, grads_ref.at[room.near(to)], out_ref.at[room.near(place)], to))
+
+    copies = []
+    onward = to_mate(6, grads_ref.at[room.group(corner)], pool.at[0], beside)
+    direct = to_mate(5, grads_ref.at[room.group(beside)], pool.at[1], beside)
     for shift in range(team):
         to = lax.rem(place + shift, team)
         copies.append(row_copy(
-            sems, team + shift, grads_ref.at[room.far(to)], out_ref.at[room.far(place)], other(shift)
+            sems, 1 + shift, grads_ref.at[room.far(to)], out_ref.at[room.far(place)], other(shift)
         ))
         copies[-1].start()
-    for shift in shifts:
-        to = lax.rem(place + shift, team)
-        copies.append(row_copy(
-            sems, 2 * team - 1 + shift, grads_ref.at[room.near(to)], out_ref.at[room.near(place)],
-            mate(shift),
-        ))
-        copies[-1].start()
-    for copy in pools:
-        copy.wait_recv()
-
-    mine = room.common + place * room.shared
-
-    @pl.loop(0, room.shared)
-    def _(index):
-        value = grads_ref[mine + index].astype(jnp.float32)
-        for part in range(team - 1):
-            value = value + pool[part, index].astype(jnp.float32)
-        total[index] = value.astype(jnp.bfloat16)
-
+    near(8, beside)
+    onward.wait_recv()
+
+    def add(first, parts, into):
+        @pl.loop(0, room.shared)
+        def _(index):
+            value = grads_ref[first + index].astype(jnp.float32)
+            for part in parts:
+                value = value + pool[part, index].astype(jnp.float32)
+            into[index] = value.astype(jnp.bfloat16)
+
+    add(room.common + across * room.shared, (0,), passing)
+    passed = to_mate(7, passing, pool.at[2], across)
+    near(9, across)
+    direct.wait_recv()
+    passed.wait_recv()
+    add(room.common + place * room.shared, (1, 2), total)
     common = pl.ds(room.common, room.shared)
     group = row_copy(sems, 0, total, out_ref.at[common], other(0))
     group.start()
-    for copy in pools:
+    near(10, corner)
+    for copy in (onward, direct, passed):
         copy.wait_send()
     own.wait()
     for copy in copies:
@@ -816,7 +901,7 @@
         got = pl.pallas_call(
             functools.partial(spread_kernel, room, n_rows),
             out_shape=spread, in_specs=[VM], out_specs=VM, compiler_params=remote(0),
-            scratch_shapes=remote_sems(3 * room.team - 1), name="spread",
+            scratch_shapes=remote_sems(11), name="spread",
         )(send)
         part = pl.pallas_call(
             functools.partial(scores_kernel, step, lambda x: room.place(x, size)),
@@ -824,7 +909,7 @@
             in_specs=[SM] * 4 + [VM, in_hbm], out_specs=VM, compiler_params=SLOTS,
             scratch_shapes=tile_room, name="scores",
         )(*scalars, got, tiles)
-        residual, loss = classify(step, n_cols, part, labels)
+        residual, loss = split_classify(step, n_cols, part, labels)
         losses.append(loss)
         grads = pl.pallas_call(
             functools.partial(grads_kernel, step, lambda x: room.place(x, size)),
@@ -837,9 +922,10 @@
             functools.partial(gather_kernel, room, n_rows),
             out_shape=packed, in_specs=[VM], out_specs=VM, compiler_params=remote(1),
             scratch_shapes=[
-                pltpu.VMEM((room.team - 1, shared, classes, size), jnp.bfloat16),
+                pltpu.VMEM((3, shared, classes, size), jnp.bfloat16),
                 pltpu.VMEM((shared, classes, size), jnp.bfloat16),
-                *remote_sems(3 * room.team - 1),
+                pltpu.VMEM((shared, classes, size), jnp.bfloat16),
+                *remote_sems(11),
             ],
             name="gather",
         )(grads)

time: 191 us -> 189 us (0.990); the launches traced: 190 us -> 192 us
  Pallas kernels: 180 us -> 186 us
  local copies, waits for them, and re-layouts: 7.3 us -> 4.34 us
    pallas_call x2, Pallas kernels: 60.9 us -> 67.9 us  [team_program(): pl.pallas_call(functools.partial(spread_kernel, room, n_rows), out_shape=...]
    pallas_call x2, Pallas kernels: 17.9 us -> 13.4 us  [split_classify(): pl.pallas_call(functools.partial(split_classify_kernel, n_cols, step), ou...]
    cond x20 -> x14, local copies, waits for them, and re-layouts: 3.01 us -> 0.04 us
    pallas_call x2, Pallas kernels: 59.3 us -> 62.1 us  [team_program(): pl.pallas_call(functools.partial(gather_kernel, room, n_rows), out_shape=...]
where the time goes in v1:
time: 189 us; the launch traced here: 192 us
  Pallas kernels  186 us (98%)
  local copies, waits for them, and re-layouts  4.34 us (2%)
    pallas_call x2, Pallas kernels, team_program(): pl.pallas_call(functools.partial(spread_kernel, room, n_rows), out_shape=...  67.9 us
    pallas_call x2, Pallas kernels, team_program(): pl.pallas_call(functools.partial(gather_kernel, room, n_rows), out_shape=...  62.1 us
    pallas_call x1, Pallas kernels, mark(): pl.pallas_call(functools.partial(mark_kernel, n_rows, n_cols, steps), out...  13.5 us
    pallas_call x2, Pallas kernels, split_classify(): pl.pallas_call(functools.partial(split_classify_kernel, n_cols, step), ou...  13.4 us
    pallas_call x2, Pallas kernels, team_program(): pl.pallas_call(functools.partial(scores_kernel, step, lambda x: room.plac...  10.1 us
    pallas_call x2, Pallas kernels, team_program(): pl.pallas_call(functools.partial(grads_kernel, step, lambda x: room.place...  7.67 us
    pallas_call x2, Pallas kernels, team_program(): pl.pallas_call(functools.partial(apply_pack_lists if more else apply_list...  6.43 us

profile of v1, /device:TPU:0, one launch (start us, length us, event | category | flops | bytes accessed | tf_op | source)
XLA Modules:
  0.0 192.3 jit_solution(555499829596951265)
XLA Ops:
  0.6 1.3 copy.20.count_ref
  1.9 13.5 %mark.1.all_ref = bf16[4,8,16,128]{3,2,1,0:T(8,128)(2,1)} custom-call(s32[2,128]{1,0:T(2,128)} %bitcast.2, s32[2,1,1]{2,1,0:T(1,128)} %copy.20.count_ref), custom_call_target="tpu_custom_call" | custom-call | tf_op jit(solution)/shard_map/mark/pallas_call | solution.py:503
  15.4 0.9 copy-done.3
  16.3 0.7 copy-done.4
  17.0 0.7 copy-done.5
  17.7 2.0 %plan.1 = (s32[2,128]{1,0:T(2,128)S(1)}, s32[2,1152]{1,0:T(2,128)S(1)}, s32[1]{0:T(128)}) custom-call(bf16[4,8,16,128]{3,2,1,0:T(8,128)(2,1)S(1)} %copy-done.3, s32[2,128]{1,0:T(2,128)S(1)} %bitcast.3, s32[2,1,1]{2,1,0:T(1,128)S(1)} %copy-done.5), custom_call_target="tpu_custom_call" | custom-call | tf_op jit(solution)/shard_map/plan/pallas_call | solution.py:606
  20.4 171.9 %conditional.1 = (f32[32,16384]{1,0:T(8,128)}, f32[2,256]{1,0:T(2,128)}) conditional(s32[]{:T(128)} %bitcast.1, (s32[2,1152]{1,0:T(2,128)S(1)}, f32[32,16384]{1,0:T(8,128)}, s32[2,128]{1,0:T(2,128)S(1)}, s32[2,1,1,128]{3,2,1,0:T(1,128)}, f32[2,1,1,128]{3,2,1,0:T(1,128)}, /*index=5*/s32[2,1,1]{0,2,1:T(1,128)}, ...), branch_computations={%region_0.0_spmd, %region_1.0_spmd, %region_2.0_spmd, %region_3.0_... | conditional | flops 512 | bytes 126398856 | solution.py:957
  20.6 0.7 copy.24.count_ref
  21.3 2.6 %pack.7.send = bf16[170,32,128]{2,1,0:T(8,128)(2,1)S(1)} custom-call(s32[2,1152]{1,0:T(2,128)S(1)} %get-tuple-element.120.lists_ref, f32[32,16384]{1,0:T(8,128)} %get-tuple-element.122.weights_ref), custom_call_target="tpu_custom_call" | custom-call | tf_op jit(solution)/shard_map/cond/branch_2_fun/pack/pallas_call | solution.py:895
  24.0 34.9 %spread.14.recv_ref = bf16[224,32,128]{2,1,0:T(8,128)(2,1)S(1)} custom-call(bf16[170,32,128]{2,1,0:T(8,128)(2,1)S(1)} %pack.7.send), custom_call_target="tpu_custom_call" | custom-call | tf_op jit(solution)/shard_map/cond/branch_2_fun/spread/pallas_call | solution.py:901
  59.0 0.0 slice-start.5
  59.0 5.2 %scores.14.part_ref = f32[32,1024]{1,0:T(8,128)S(1)} custom-call(s32[2,128]{1,0:T(2,128)S(1)} %get-tuple-element.123.code_ref, s32[2,1,1,128]{3,2,1,0:T(1,128)S(1)} %copy-done.18, f32[2,1,1,128]{3,2,1,0:T(1,128)S(1)} %copy-done.23, s32[2,1,1]{2,1,0:T(1,128)S(1)} %copy.24.count_ref, bf16[224,32,128]{2,1,0:T(8,128)(2,1)S(1)} %spread.14.recv_ref, ...), custom_call_target="tpu_custom_call" | custom-call | tf_op jit(solution)/shard_map/cond/branch_2_fun/scores/pallas_call | solution.py:906
  64.2 6.2 %classify.14 = (bf16[32,1024]{1,0:T(8,128)(2,1)S(1)}, f32[1,256]{1,0:T(1,128)S(1)}) custom-call(f32[32,1024]{1,0:T(8,128)S(1)} %scores.14.part_ref, s32[2,1024]{1,0:T(2,128)S(1)} %copy-done.13), custom_call_target="tpu_custom_call" | custom-call | tf_op jit(solution)/shard_map/cond/branch_2_fun/classify/pallas_call | solution.py:673
  70.4 3.5 %grads.14.grads_ref = bf16[224,32,128]{2,1,0:T(8,128)(2,1)S(1)} custom-call(s32[2,128]{1,0:T(2,128)S(1)} %get-tuple-element.123.code_ref, s32[2,1,1,128]{3,2,1,0:T(1,128)S(1)} %copy-done.18, f32[2,1,1,128]{3,2,1,0:T(1,128)S(1)} %copy-done.23, s32[2,1,1]{2,1,0:T(1,128)S(1)} %copy.24.count_ref, bf16[32,1024]{1,0:T(8,128)(2,1)S(1)} %get-tuple-element.129.residual_ref, ...), custom_call_target="tpu_custom_call" | custom-call | tf_op jit(solution)/shard_map/cond/branch_2_fun/grads/pallas_call | solution.py:914
  74.0 0.0 copy-start.8
  74.0 31.7 %gather.14.grads_ref = bf16[170,32,128]{2,1,0:T(8,128)(2,1)S(1)} custom-call(bf16[224,32,128]{2,1,0:T(8,128)(2,1)S(1)} %grads.14.grads_ref), custom_call_target="tpu_custom_call" | custom-call | tf_op jit(solution)/shard_map/cond/branch_2_fun/gather/pallas_call | solution.py:921
  105.7 3.0 %apply.14 = (f32[32,16384]{1,0:T(8,128)S(1)}, bf16[170,32,128]{2,1,0:T(8,128)(2,1)S(1)}) custom-call(s32[2,1152]{1,0:T(2,128)S(1)} %get-tuple-element.120.lists_ref, f32[2]{0:T(128)S(1)} %copy-done.28, f32[32,16384]{1,0:T(8,128)S(1)} %copy-done.8, bf16[170,32,128]{2,1,0:T(8,128)(2,1)S(1)} %gather.14.grads_ref), custom_call_target="tpu_custom_call" | custom-call | tf_op jit(solution)/shard_map/cond/branch_2_fun/apply/pallas_call | solution.py:934
  108.7 32.9 %spread.15.recv_ref = bf16[224,32,128]{2,1,0:T(8,128)(2,1)S(1)} custom-call(bf16[170,32,128]{2,1,0:T(8,128)(2,1)S(1)} %get-tuple-element.131.send), custom_call_target="tpu_custom_call" | custom-call | tf_op jit(solution)/shard_map/cond/branch_2_fun/spread/pallas_call | solution.py:901
  141.6 4.9 %scores.15.part_ref = f32[32,1024]{1,0:T(8,128)S(1)} custom-call(s32[2,128]{1,0:T(2,128)S(1)} %get-tuple-element.123.code_ref, s32[2,1,1,128]{3,2,1,0:T(1,128)S(1)} %copy-done.18, f32[2,1,1,128]{3,2,1,0:T(1,128)S(1)} %copy-done.23, s32[2,1,1]{2,1,0:T(1,128)S(1)} %copy.24.count_ref, bf16[224,32,128]{2,1,0:T(8,128)(2,1)S(1)} %spread.15.recv_ref, ...), custom_call_target="tpu_custom_call" | custom-call | tf_op jit(solution)/shard_map/cond/branch_2_fun/scores/pallas_call | solution.py:906
  146.5 7.2 %classify.15 = (bf16[32,1024]{1,0:T(8,128)(2,1)S(1)}, f32[1,256]{1,0:T(1,128)S(1)}) custom-call(f32[32,1024]{1,0:T(8,128)S(1)} %scores.15.part_ref, s32[2,1024]{1,0:T(2,128)S(1)} %copy-done.13), custom_call_target="tpu_custom_call" | custom-call | tf_op jit(solution)/shard_map/cond/branch_2_fun/classify/pallas_call | solution.py:673
  153.7 0.6 pad_maximum_fusion.2
  154.3 4.1 %grads.15.grads_ref = bf16[224,32,128]{2,1,0:T(8,128)(2,1)S(1)} custom-call(s32[2,128]{1,0:T(2,128)S(1)} %get-tuple-element.123.code_ref, s32[2,1,1,128]{3,2,1,0:T(1,128)S(1)} %copy-done.18, f32[2,1,1,128]{3,2,1,0:T(1,128)S(1)} %copy-done.23, s32[2,1,1]{2,1,0:T(1,128)S(1)} %copy.24.count_ref, bf16[32,1024]{1,0:T(8,128)(2,1)S(1)} %get-tuple-element.132.residual_ref, ...), custom_call_target="tpu_custom_call" | custom-call | tf_op jit(solution)/shard_map/cond/branch_2_fun/grads/pallas_call | solution.py:914
  158.4 30.5 %gather.15.grads_ref = bf16[170,32,128]{2,1,0:T(8,128)(2,1)S(1)} custom-call(bf16[224,32,128]{2,1,0:T(8,128)(2,1)S(1)} %grads.15.grads_ref), custom_call_target="tpu_custom_call" | custom-call | tf_op jit(solution)/shard_map/cond/branch_2_fun/gather/pallas_call | solution.py:921
  188.9 3.4 %apply.15 = f32[32,16384]{1,0:T(8,128)} custom-call(s32[2,1152]{1,0:T(2,128)S(1)} %get-tuple-element.120.lists_ref, f32[2]{0:T(128)S(1)} %copy-done.28, f32[32,16384]{1,0:T(8,128)S(1)} %get-tuple-element.130.weights_ref, bf16[170,32,128]{2,1,0:T(8,128)(2,1)S(1)} %gather.15.grads_ref), custom_call_target="tpu_custom_call" | custom-call | tf_op jit(solution)/shard_map/cond/branch_2_fun/apply/pallas_call | solution.py:934
  (16 shorter events, 0.0 us)
Async XLA Ops:
  15.4 0.9 copy-start.3
  16.3 0.7 copy-start.4
  17.0 0.7 copy-start.5
  21.3 49.0 %slice-start.4 = ((s8[8388608]{0:T(1024)(128)(4,1)}), s8[4194304]{0:T(1024)(128)(4,1)S(1)}, s32[]{:S(2)}) async-start(s8[8388608]{0:T(1024)(128)(4,1)} %bitcast.8), calls=%async_computation.4 | async-start | bytes 8388608 | tf_op jit(solution)/shard_map/cond
  24.0 35.0 %copy-start.18 = (s32[2,1,1,128]{3,2,1,0:T(1,128)S(1)}, s32[2,1,1,128]{3,2,1,0:T(1,128)}, u32[]{:S(2)}) copy-start(s32[2,1,1,128]{3,2,1,0:T(1,128)} %get-tuple-element.124.row_ref) | copy-start | bytes 3076 | tf_op jit(solution)/shard_map/cond
  24.0 35.0 %copy-start.23 = (f32[2,1,1,128]{3,2,1,0:T(1,128)S(1)}, f32[2,1,1,128]{3,2,1,0:T(1,128)}, u32[]{:S(2)}) copy-start(f32[2,1,1,128]{3,2,1,0:T(1,128)} %get-tuple-element.125.scale_ref) | copy-start | bytes 3076 | tf_op jit(solution)/shard_map/cond
  58.9 5.2 %copy-start.13 = (s32[2,1024]{1,0:T(2,128)S(1)}, s32[2,1024]{1,0:T(2,128)}, u32[]{:S(2)}) copy-start(s32[2,1024]{1,0:T(2,128)} %get-tuple-element.128.labels_ref) | copy-start | bytes 24580 | tf_op jit(solution)/shard_map/cond
  59.0 11.4 %slice-start.5 = ((s8[8388608]{0:T(1024)(128)(4,1)}), s8[4194304]{0:T(1024)(128)(4,1)S(1)}, s32[]{:S(2)}) async-start(s8[8388608]{0:T(1024)(128)(4,1)} %bitcast.8), calls=%async_computation.5 | async-start | bytes 8388608 | tf_op jit(solution)/shard_map/cond
  74.0 31.7 %copy-start.8 = (f32[32,16384]{1,0:T(8,128)S(1)}, f32[32,16384]{1,0:T(8,128)}, u32[]{:S(2)}) copy-start(f32[32,16384]{1,0:T(8,128)} %get-tuple-element.122.weights_ref) | copy-start | bytes 6291460 | tf_op jit(solution)/shard_map/cond
  74.0 31.7 %copy-start.28 = (f32[2]{0:T(128)S(1)}, f32[2]{0:T(128)}, u32[]{:S(2)}) copy-start(f32[2]{0:T(128)} %get-tuple-element.121.rate_ref) | copy-start | bytes 28 | tf_op jit(solution)/shard_map/cond

commit v2 on v1

--- a/solution.py
+++ b/solution.py
@@ -166,7 +166,8 @@
 
 def slot_scalars(step, place_of, slot, code_ref, row_ref, scale_ref, count_ref):
     place = place_of(code_ref[step, slot])
-    factor = jnp.where(slot < count_ref[step, 0, 0], scale_ref[step, 0, 0, slot], 0.0)
+    count = count_ref[(step,) + (0,) * (len(count_ref.shape) - 1)]
+    factor = jnp.where(slot < count, scale_ref[step, 0, 0, slot], 0.0)
     return place, row_ref[step, 0, 0, slot], factor
 
 
@@ -411,7 +412,7 @@
 
 
 SPILL = 12
-TIERS = ((23, 14), (24, 16), (26, 18), (28, 22))
+TIERS = ((23, 14), (24, 16), (26, 18), (28, 21), (32, 26))
 LEFT_RIGHT = (((1,), (1,)), ((), ()))
 
 
@@ -436,13 +437,9 @@
     return lambda: pl.semaphore_wait(barrier, len(peers))
 
 
-def slots_of(tile_cols, count, steps):
-    slots = tile_cols.shape[1]
-    ids = lax.broadcasted_iota(jnp.int32, (1, slots), 1)
-    return [(tile_cols[s : s + 1, :], ids < count(s)) for s in range(steps)]
-
-
-def mark_kernel(n_rows, n_cols, steps, cols_ref, count_ref, all_ref, mine, send_sems, recv_sems, own_sem):
+def mark_kernel(
+    n_rows, n_cols, steps, cols_ref, count_ref, all_ref, live_ref, mine, send_sems, recv_sems, own_sem
+):
     row, col = lax.axis_index("rows"), lax.axis_index("cols")
     row_peers = [lax.rem(row + shift, n_rows) for shift in range(1, n_rows)]
     col_peers = [lax.rem(col + shift, n_cols) for shift in range(1, n_cols)]
@@ -453,11 +450,14 @@
         pl.semaphore_signal(barrier, inc=1, device_id={"cols": peer}, device_id_type=MESH)
     size = mine.shape[1]
     marks = []
-    for cols, live in slots_of(cols_ref[...], lambda s: count_ref[s, 0, 0], steps):
-        slots = cols.shape[1]
+    slots = cols_ref.shape[1]
+    ids = lax.broadcasted_iota(jnp.int32, (1, slots), 1)
+    for s in range(steps):
+        cols = jnp.where(ids < count_ref[s], cols_ref[s : s + 1, :], -1)
+        live_ref[s : s + 1, :] = cols
         owners = lax.broadcasted_iota(jnp.int32, (n_rows, slots), 0)
         places = lax.broadcasted_iota(jnp.int32, (size, slots), 0)
-        first = jnp.where(live & (cols >> 7 == owners), 1.0, 0.0).astype(jnp.bfloat16)
+        first = jnp.where(cols >> 7 == owners, 1.0, 0.0).astype(jnp.bfloat16)
         second = jnp.where((cols & 127) == places, 1.0, 0.0).astype(jnp.bfloat16)
         count = lax.dot_general(first, second, LEFT_RIGHT, preferred_element_type=jnp.float32)
         marks.append(jnp.minimum(count, 1.0))
@@ -478,23 +478,32 @@
             )
         )
         copies[-1].start()
+    onward = []
+
+    def hand_on(shift):
+        piece = all_ref.at[col, lax.rem(row + n_rows - shift, n_rows)]
+        for index, peer in enumerate(col_peers):
+            at = n_rows + shift * (n_cols - 1) + index
+            onward.append(
+                pltpu.make_async_remote_copy(
+                    src_ref=mine if shift == 0 else piece,
+                    dst_ref=piece,
+                    send_sem=send_sems.at[at],
+                    recv_sem=recv_sems.at[at],
+                    device_id={"cols": peer},
+                    device_id_type=MESH,
+                )
+            )
+            onward[-1].start()
+
+    hand_on(0)
+    for index, copy in enumerate(copies):
+        copy.wait_recv()
+        hand_on(index + 1)
     own.wait()
     for copy in copies:
-        copy.wait()
-    copies = []
-    for index, peer in enumerate(col_peers):
-        copies.append(
-            pltpu.make_async_remote_copy(
-                src_ref=all_ref.at[col],
-                dst_ref=all_ref.at[col],
-                send_sem=send_sems.at[n_rows + index],
-                recv_sem=recv_sems.at[n_rows + index],
-                device_id={"cols": peer},
-                device_id_type=MESH,
-            )
-        )
-        copies[-1].start()
-    for copy in copies:
+        copy.wait_send()
+    for copy in onward:
         copy.wait()
 
 
@@ -502,13 +511,16 @@
     steps = tile_cols.shape[0]
     return pl.pallas_call(
         functools.partial(mark_kernel, n_rows, n_cols, steps),
-        out_shape=jax.ShapeDtypeStruct((n_cols, n_rows, steps * n_rows, size), jnp.bfloat16),
+        out_shape=(
+            jax.ShapeDtypeStruct((n_cols, n_rows, steps * n_rows, size), jnp.bfloat16),
+            jax.ShapeDtypeStruct(tile_cols.shape, jnp.int32),
+        ),
         in_specs=[VM, SM],
-        out_specs=VM,
+        out_specs=(VM, VM),
         scratch_shapes=[
             pltpu.VMEM((steps * n_rows, size), jnp.bfloat16),
-            pltpu.SemaphoreType.DMA((n_rows + n_cols,)),
-            pltpu.SemaphoreType.DMA((n_rows + n_cols,)),
+            pltpu.SemaphoreType.DMA((n_rows * n_cols,)),
+            pltpu.SemaphoreType.DMA((n_rows * n_cols,)),
             pltpu.SemaphoreType.DMA,
         ],
         compiler_params=pltpu.CompilerParams(collective_id=0, has_side_effects=True),
@@ -517,8 +529,15 @@
 
 
 def plan_kernel(
-    n_rows, steps, all_ref, cols_ref, count_ref, code_ref, list_ref, tier_ref, keys, shared_keys, table
-):
+    n_rows, steps, all_hbm, cols_hbm, code_ref, list_ref, tier_ref, all_ref, cols_ref, keys,
+    shared_keys, table, sems
+):
+    fetch = [
+        pltpu.make_async_copy(all_hbm, all_ref, sems.at[0]),
+        pltpu.make_async_copy(cols_hbm, cols_ref, sems.at[1]),
+    ]
+    for copy in fetch:
+        copy.start()
     team, row, half, _, _, _ = teams(n_rows)
     col = lax.axis_index("cols")
     size = all_ref.shape[-1]
@@ -533,6 +552,9 @@
         return jnp.dot(flat, triangle, preferred_element_type=jnp.float32).reshape(flags.shape)
 
     owner = lax.rem(lax.broadcasted_iota(jnp.int32, (1, depth, size), 1), n_rows)
+    table[...] = jnp.full_like(table, -1.0)
+    for copy in fetch:
+        copy.wait()
     most_listed, most_shared = [], []
     for part in range(2):
         needs = all_ref[:, part * team : (part + 1) * team].astype(jnp.float32)
@@ -561,7 +583,6 @@
         tier = tier + jnp.where((listed > cap) | (shared > shared_cap), 1, 0).astype(jnp.int32)
     tier_ref[0] = tier
 
-    table[...] = jnp.full_like(table, -1.0)
     sub = lax.broadcasted_iota(jnp.int32, (n_rows, size), 0)
     slot = lax.rem(sub, team)
     n_lists = 2 * team + 1
@@ -590,16 +611,17 @@
             hit = flipped[:, at : at + 1] == lane
             picked = jnp.sum(jnp.where(hit, down, 0.0), axis=0, keepdims=True)
             list_ref[s : s + 1, index * size : (index + 1) * size] = picked.astype(jnp.int32)
-    for s, (cols, live) in enumerate(slots_of(cols_ref[...], lambda s: count_ref[s, 0, 0], steps)):
+    for s in range(steps):
+        cols = cols_ref[s : s + 1, :]
         chosen = jnp.zeros((size, size), jnp.float32)
         for index in range(n_rows):
             at = 2 * n_rows * steps + s * n_rows + index
             chosen = jnp.where(cols >> 7 == index, flipped[:, at : at + 1], chosen)
         code = jnp.sum(jnp.where((cols & 127) == before, chosen, 0.0), axis=0, keepdims=True)
-        code_ref[s : s + 1, :] = jnp.where(live, code, 0.0).astype(jnp.int32)
-
-
-def plan(everyone, tile_cols, tile_counts, n_rows):
+        code_ref[s : s + 1, :] = jnp.where(cols >= 0, code, 0.0).astype(jnp.int32)
+
+
+def plan(everyone, tile_cols, n_rows):
     steps, slots = tile_cols.shape
     size = everyone.shape[-1]
     lists = n_rows + 1
@@ -610,16 +632,19 @@
             jax.ShapeDtypeStruct((steps, lists * size), jnp.int32),
             jax.ShapeDtypeStruct((1,), jnp.int32),
         ),
-        in_specs=[VM, VM, SM],
+        in_specs=[pl.BlockSpec(memory_space=pltpu.HBM)] * 2,
         out_specs=(VM, VM, SM),
         scratch_shapes=[
+            pltpu.VMEM(everyone.shape, everyone.dtype),
+            pltpu.VMEM(tile_cols.shape, tile_cols.dtype),
             pltpu.VMEM(everyone.shape, jnp.float32),
             pltpu.VMEM((everyone.shape[0], 2, *everyone.shape[2:]), jnp.float32),
             pltpu.VMEM((size, size), jnp.float32),
+            pltpu.SemaphoreType.DMA((2,)),
         ],
-        compiler_params=LOCAL,
+        compiler_params=pltpu.CompilerParams(vmem_limit_bytes=67_000_000),
         name="plan",
-    )(everyone, tile_cols, tile_counts)
+    )(everyone, tile_cols)
 
 
 def split_classify_kernel(
@@ -789,11 +814,11 @@
         ))
         copies[-1].start()
     to_mate(8, send.at[room.near(beside)], room.near(place), beside)
+    to_mate(9, send.at[room.near(across)], room.near(place), across)
     group.wait_recv()
     mine = room.group(place)
     passed = to_mate(6, got_ref.at[mine], mine, across)
     to_mate(5, got_ref.at[mine], mine, beside)
-    to_mate(9, send.at[room.near(across)], room.near(place), across)
     to_mate(10, send.at[room.near(corner)], room.near(place), corner)
 
     passed.wait_recv()
@@ -836,6 +861,7 @@
         ))
         copies[-1].start()
     near(8, beside)
+    near(9, across)
     onward.wait_recv()
 
     def add(first, parts, into):
@@ -848,7 +874,6 @@
 
     add(room.common + across * room.shared, (0,), passing)
     passed = to_mate(7, passing, pool.at[2], across)
-    near(9, across)
     direct.wait_recv()
     passed.wait_recv()
     add(room.common + place * room.shared, (1, 2), total)
@@ -948,8 +973,10 @@
     size = tiles.shape[-1]
     n_rows, n_cols = lax.axis_size("rows"), lax.axis_size("cols")
     cols = tile_cols[:, 0, 0]
-    everyone = mark(cols, tile_counts, n_rows, n_cols, size)
-    code, lists, tier = plan(everyone, cols, tile_counts, n_rows)
+    counts = tile_counts[:, 0, 0]
+    everyone, live = mark(cols, counts, n_rows, n_cols, size)
+    code, lists, tier = plan(everyone, live, n_rows)
+    args = (*args[:4], counts, *args[5:])
     branches = [
         functools.partial(team_program, n_rows, listed, shared, branch)
         for branch, (listed, shared) in enumerate((*TIERS, (size, size)))

time: 189 us -> 181 us (0.958); the launches traced: 192 us -> 177 us
  Pallas kernels: 186 us -> 175 us
  local copies, waits for them, and re-layouts: 4.34 us -> 0.05 us
    pallas_call x2, Pallas kernels: 67.9 us -> 60.5 us  [team_program(): pl.pallas_call(functools.partial(spread_kernel, room, n_rows), out_shape=...]
    unnamed x7 -> x0, local copies, waits for them, and re-layouts: 3.55 us -> none
    pallas_call x2, Pallas kernels: 62.1 us -> 59.7 us  [team_program(): pl.pallas_call(functools.partial(gather_kernel, room, n_rows), out_shape=...]
where the time goes in v2:
time: 181 us; the launch traced here: 177 us
  Pallas kernels  175 us (97%)
    pallas_call x2, Pallas kernels, team_program(): pl.pallas_call(functools.partial(spread_kernel, room, n_rows), out_shape=...  60.5 us
    pallas_call x2, Pallas kernels, team_program(): pl.pallas_call(functools.partial(gather_kernel, room, n_rows), out_shape=...  59.7 us
    pallas_call x1, Pallas kernels, mark(): pl.pallas_call(functools.partial(mark_kernel, n_rows, n_cols, steps), out...  14 us
    pallas_call x2, Pallas kernels, split_classify(): pl.pallas_call(functools.partial(split_classify_kernel, n_cols, step), ou...  13.5 us
    pallas_call x2, Pallas kernels, team_program(): pl.pallas_call(functools.partial(scores_kernel, step, lambda x: room.plac...  9.31 us
    pallas_call x2, Pallas kernels, team_program(): pl.pallas_call(functools.partial(grads_kernel, step, lambda x: room.place...  7.05 us
    pallas_call x2, Pallas kernels, team_program(): pl.pallas_call(functools.partial(apply_pack_lists if more else apply_list...  6.22 us

profile of v2, /device:TPU:0, one launch (start us, length us, event | category | flops | bytes accessed | tf_op | source)
XLA Modules:
  0.0 177.4 jit_solution(4657151961420060996)
XLA Ops:
  0.6 14.0 %mark.1 = (bf16[4,8,16,128]{3,2,1,0:T(8,128)(2,1)}, s32[2,128]{1,0:T(2,128)}) custom-call(s32[2,128]{1,0:T(2,128)} %bitcast.22, s32[2]{0:T(128)} %bitcast.15), custom_call_target="tpu_custom_call" | custom-call | tf_op jit(solution)/shard_map/mark/pallas_call | solution.py:512
  14.6 2.4 %plan.1 = (s32[2,128]{1,0:T(2,128)S(1)}, s32[2,1152]{1,0:T(2,128)S(1)}, s32[1]{0:T(128)}) custom-call(bf16[4,8,16,128]{3,2,1,0:T(8,128)(2,1)} %get-tuple-element.205.all_hbm, s32[2,128]{1,0:T(2,128)} %get-tuple-element.206.cols_hbm), custom_call_target="tpu_custom_call" | custom-call | tf_op jit(solution)/shard_map/plan/pallas_call | solution.py:628
  17.6 159.7 %conditional.1 = (f32[32,16384]{1,0:T(8,128)}, f32[2,256]{1,0:T(2,128)}) conditional(s32[]{:T(128)} %bitcast.2, (s32[2,1152]{1,0:T(2,128)S(1)}, f32[32,16384]{1,0:T(8,128)}, s32[2,128]{1,0:T(2,128)S(1)}, s32[2,1,1,128]{3,2,1,0:T(1,128)}, f32[2,1,1,128]{3,2,1,0:T(1,128)}, /*index=5*/s32[2]{0:T(128)}, ...), branch_computations={%region_0.0_spmd, %region_1.0_spmd, %region_2.0_spmd, %region_3.0_... | conditional | flops 512 | bytes 101233016 | solution.py:984
  17.7 0.0 slice-start.2
  17.7 2.6 %pack.7.send = bf16[160,32,128]{2,1,0:T(8,128)(2,1)S(1)} custom-call(s32[2,1152]{1,0:T(2,128)S(1)} %get-tuple-element.123.lists_ref, f32[32,16384]{1,0:T(8,128)} %get-tuple-element.125.weights_ref), custom_call_target="tpu_custom_call" | custom-call | tf_op jit(solution)/shard_map/cond/branch_1_fun/pack/pallas_call | solution.py:920
  20.3 0.0 copy-start.16
  20.3 0.0 copy-start.22
  20.3 0.0 copy-start.28
  20.3 32.2 %spread.14.recv_ref = bf16[208,32,128]{2,1,0:T(8,128)(2,1)S(1)} custom-call(bf16[160,32,128]{2,1,0:T(8,128)(2,1)S(1)} %pack.7.send), custom_call_target="tpu_custom_call" | custom-call | tf_op jit(solution)/shard_map/cond/branch_1_fun/spread/pallas_call | solution.py:926
  52.5 0.0 copy-start.10
  52.5 0.0 slice-start.3
  52.5 5.2 %scores.14.part_ref = f32[32,1024]{1,0:T(8,128)S(1)} custom-call(s32[2,128]{1,0:T(2,128)S(1)} %get-tuple-element.126.code_ref, s32[2,1,1,128]{3,2,1,0:T(1,128)S(1)} %copy-done.16, f32[2,1,1,128]{3,2,1,0:T(1,128)S(1)} %copy-done.22, s32[2]{0:T(128)S(1)} %copy-done.28, bf16[208,32,128]{2,1,0:T(8,128)(2,1)S(1)} %spread.14.recv_ref, ...), custom_call_target="tpu_custom_call" | custom-call | tf_op jit(solution)/shard_map/cond/branch_1_fun/scores/pallas_call | solution.py:931
  57.7 6.2 %classify.14 = (bf16[32,1024]{1,0:T(8,128)(2,1)S(1)}, f32[1,256]{1,0:T(1,128)S(1)}) custom-call(f32[32,1024]{1,0:T(8,128)S(1)} %scores.14.part_ref, s32[2,1024]{1,0:T(2,128)S(1)} %copy-done.10), custom_call_target="tpu_custom_call" | custom-call | tf_op jit(solution)/shard_map/cond/branch_1_fun/classify/pallas_call | solution.py:698
  64.0 3.5 %grads.14.grads_ref = bf16[208,32,128]{2,1,0:T(8,128)(2,1)S(1)} custom-call(s32[2,128]{1,0:T(2,128)S(1)} %get-tuple-element.126.code_ref, s32[2,1,1,128]{3,2,1,0:T(1,128)S(1)} %copy-done.16, f32[2,1,1,128]{3,2,1,0:T(1,128)S(1)} %copy-done.22, s32[2]{0:T(128)S(1)} %copy-done.28, bf16[32,1024]{1,0:T(8,128)(2,1)S(1)} %get-tuple-element.132.residual_ref, ...), custom_call_target="tpu_custom_call" | custom-call | tf_op jit(solution)/shard_map/cond/branch_1_fun/grads/pallas_call | solution.py:939
  67.5 0.0 copy-start.4
  67.5 29.4 %gather.14.grads_ref = bf16[160,32,128]{2,1,0:T(8,128)(2,1)S(1)} custom-call(bf16[208,32,128]{2,1,0:T(8,128)(2,1)S(1)} %grads.14.grads_ref), custom_call_target="tpu_custom_call" | custom-call | tf_op jit(solution)/shard_map/cond/branch_1_fun/gather/pallas_call | solution.py:946
  97.0 2.9 %apply.14 = (f32[32,16384]{1,0:T(8,128)S(1)}, bf16[160,32,128]{2,1,0:T(8,128)(2,1)S(1)}) custom-call(s32[2,1152]{1,0:T(2,128)S(1)} %get-tuple-element.123.lists_ref, f32[2]{0:T(128)S(1)} %copy-done.34, f32[32,16384]{1,0:T(8,128)S(1)} %copy-done.4, bf16[160,32,128]{2,1,0:T(8,128)(2,1)S(1)} %gather.14.grads_ref), custom_call_target="tpu_custom_call" | custom-call | tf_op jit(solution)/shard_map/cond/branch_1_fun/apply/pallas_call | solution.py:959
  99.9 28.3 %spread.15.recv_ref = bf16[208,32,128]{2,1,0:T(8,128)(2,1)S(1)} custom-call(bf16[160,32,128]{2,1,0:T(8,128)(2,1)S(1)} %get-tuple-element.134.send), custom_call_target="tpu_custom_call" | custom-call | tf_op jit(solution)/shard_map/cond/branch_1_fun/spread/pallas_call | solution.py:926
  128.2 4.1 %scores.15.part_ref = f32[32,1024]{1,0:T(8,128)S(1)} custom-call(s32[2,128]{1,0:T(2,128)S(1)} %get-tuple-element.126.code_ref, s32[2,1,1,128]{3,2,1,0:T(1,128)S(1)} %copy-done.16, f32[2,1,1,128]{3,2,1,0:T(1,128)S(1)} %copy-done.22, s32[2]{0:T(128)S(1)} %copy-done.28, bf16[208,32,128]{2,1,0:T(8,128)(2,1)S(1)} %spread.15.recv_ref, ...), custom_call_target="tpu_custom_call" | custom-call | tf_op jit(solution)/shard_map/cond/branch_1_fun/scores/pallas_call | solution.py:931
  132.3 7.3 %classify.15 = (bf16[32,1024]{1,0:T(8,128)(2,1)S(1)}, f32[1,256]{1,0:T(1,128)S(1)}) custom-call(f32[32,1024]{1,0:T(8,128)S(1)} %scores.15.part_ref, s32[2,1024]{1,0:T(2,128)S(1)} %copy-done.10), custom_call_target="tpu_custom_call" | custom-call | tf_op jit(solution)/shard_map/cond/branch_1_fun/classify/pallas_call | solution.py:698
  139.6 0.6 pad_maximum_fusion.1
  140.2 3.6 %grads.15.grads_ref = bf16[208,32,128]{2,1,0:T(8,128)(2,1)S(1)} custom-call(s32[2,128]{1,0:T(2,128)S(1)} %get-tuple-element.126.code_ref, s32[2,1,1,128]{3,2,1,0:T(1,128)S(1)} %copy-done.16, f32[2,1,1,128]{3,2,1,0:T(1,128)S(1)} %copy-done.22, s32[2]{0:T(128)S(1)} %copy-done.28, bf16[32,1024]{1,0:T(8,128)(2,1)S(1)} %get-tuple-element.135.residual_ref, ...), custom_call_target="tpu_custom_call" | custom-call | tf_op jit(solution)/shard_map/cond/branch_1_fun/grads/pallas_call | solution.py:939
  143.8 30.3 %gather.15.grads_ref = bf16[160,32,128]{2,1,0:T(8,128)(2,1)S(1)} custom-call(bf16[208,32,128]{2,1,0:T(8,128)(2,1)S(1)} %grads.15.grads_ref), custom_call_target="tpu_custom_call" | custom-call | tf_op jit(solution)/shard_map/cond/branch_1_fun/gather/pallas_call | solution.py:946
  174.0 3.3 %apply.15 = f32[32,16384]{1,0:T(8,128)} custom-call(s32[2,1152]{1,0:T(2,128)S(1)} %get-tuple-element.123.lists_ref, f32[2]{0:T(128)S(1)} %copy-done.34, f32[32,16384]{1,0:T(8,128)S(1)} %get-tuple-element.133.weights_ref, bf16[160,32,128]{2,1,0:T(8,128)(2,1)S(1)} %gather.15.grads_ref), custom_call_target="tpu_custom_call" | custom-call | tf_op jit(solution)/shard_map/cond/branch_1_fun/apply/pallas_call | solution.py:959
  (10 shorter events, 0.0 us)
Async XLA Ops:
  17.7 46.3 %slice-start.2 = ((s8[8388608]{0:T(1024)(128)(4,1)}), s8[4194304]{0:T(1024)(128)(4,1)S(1)}, s32[]{:S(2)}) async-start(s8[8388608]{0:T(1024)(128)(4,1)} %bitcast.5), calls=%async_computation.2 | async-start | bytes 8388608 | tf_op jit(solution)/shard_map/cond
  20.3 32.2 %copy-start.16 = (s32[2,1,1,128]{3,2,1,0:T(1,128)S(1)}, s32[2,1,1,128]{3,2,1,0:T(1,128)}, u32[]{:S(2)}) copy-start(s32[2,1,1,128]{3,2,1,0:T(1,128)} %get-tuple-element.127.row_ref) | copy-start | bytes 3076 | tf_op jit(solution)/shard_map/cond
  20.3 32.2 %copy-start.22 = (f32[2,1,1,128]{3,2,1,0:T(1,128)S(1)}, f32[2,1,1,128]{3,2,1,0:T(1,128)}, u32[]{:S(2)}) copy-start(f32[2,1,1,128]{3,2,1,0:T(1,128)} %get-tuple-element.128.scale_ref) | copy-start | bytes 3076 | tf_op jit(solution)/shard_map/cond
  20.3 32.2 %copy-start.28 = (s32[2]{0:T(128)S(1)}, s32[2]{0:T(128)}, u32[]{:S(2)}) copy-start(s32[2]{0:T(128)} %get-tuple-element.129.count_ref) | copy-start | bytes 28 | tf_op jit(solution)/shard_map/cond
  52.5 5.2 %copy-start.10 = (s32[2,1024]{1,0:T(2,128)S(1)}, s32[2,1024]{1,0:T(2,128)}, u32[]{:S(2)}) copy-start(s32[2,1024]{1,0:T(2,128)} %get-tuple-element.131.labels_ref) | copy-start | bytes 24580 | tf_op jit(solution)/shard_map/cond
  52.5 11.4 %slice-start.3 = ((s8[8388608]{0:T(1024)(128)(4,1)}), s8[4194304]{0:T(1024)(128)(4,1)S(1)}, s32[]{:S(2)}) async-start(s8[8388608]{0:T(1024)(128)(4,1)} %bitcast.5), calls=%async_computation.3 | async-start | bytes 8388608 | tf_op jit(solution)/shard_map/cond
  67.5 29.5 %copy-start.4 = (f32[32,16384]{1,0:T(8,128)S(1)}, f32[32,16384]{1,0:T(8,128)}, u32[]{:S(2)}) copy-start(f32[32,16384]{1,0:T(8,128)} %get-tuple-element.125.weights_ref) | copy-start | bytes 6291460 | tf_op jit(solution)/shard_map/cond
  67.5 29.5 %copy-start.34 = (f32[2]{0:T(128)S(1)}, f32[2]{0:T(128)}, u32[]{:S(2)}) copy-start(f32[2]{0:T(128)} %get-tuple-element.124.rate_ref) | copy-start | bytes 28 | tf_op jit(solution)/shard_map/cond

commit v3 on v2

--- a/solution.py
+++ b/solution.py
@@ -172,6 +172,9 @@
 
 
 def fetch_tiles(step, tiles_ref, held_ref, sems):
+    if sems is None:
+        return lambda group: None
+
     def copy(group):
         part = pl.ds(group * GROUP, GROUP)
         return pltpu.make_async_copy(
@@ -722,6 +725,7 @@
         self.common = self.spill + team * SPILL
         self.packed = self.common + shared
         self.spread = self.common + team * shared
+        self.limit = (16 if shared < 64 else 48) * 1024 * 1024
 
     def near(self, index):
         return pl.ds(index * self.listed, self.listed)
@@ -893,6 +897,23 @@
     return [pltpu.SemaphoreType.DMA((count,)), pltpu.SemaphoreType.DMA((count,)), pltpu.SemaphoreType.DMA]
 
 
+def resident_scores(step, place_of, code_ref, row_ref, scale_ref, count_ref, recv_ref, tiles_ref, out_ref):
+    held_ref = tiles_ref.at[step, 0, 0]
+    scores_kernel(
+        step, place_of, code_ref, row_ref, scale_ref, count_ref, recv_ref, None, out_ref, held_ref, None
+    )
+
+
+def resident_grads(
+    step, place_of, code_ref, row_ref, scale_ref, count_ref, residual_ref, tiles_ref, out_ref, total
+):
+    held_ref = tiles_ref.at[step, 0, 0]
+    grads_kernel(
+        step, place_of, code_ref, row_ref, scale_ref, count_ref, residual_ref, None, out_ref, total,
+        held_ref, None,
+    )
+
+
 def team_program(
     n_rows, listed, shared, branch, code, lists,
     tiles, tile_scales, tile_rows, tile_cols, tile_counts, labels, learning_rate, weights
@@ -907,13 +928,13 @@
     packed = jax.ShapeDtypeStruct((room.packed, classes, size), jnp.bfloat16)
     spread = jax.ShapeDtypeStruct((room.spread, classes, size), jnp.bfloat16)
     scalars = (code, tile_rows, tile_scales, tile_counts)
-    in_hbm = pl.BlockSpec(memory_space=pltpu.HBM)
     tile_room = [pltpu.VMEM(tiles.shape[3:], tiles.dtype), pltpu.SemaphoreType.DMA((slots // GROUP,))]
+    slots_params = pltpu.CompilerParams(vmem_limit_bytes=room.limit)
 
     def remote(index):
         return pltpu.CompilerParams(
             collective_id=1 + steps + 2 * branch + index, has_side_effects=True,
-            vmem_limit_bytes=VMEM_LIMIT,
+            vmem_limit_bytes=room.limit,
         )
 
     current = weights
@@ -929,18 +950,21 @@
             scratch_shapes=remote_sems(11), name="spread",
         )(send)
         part = pl.pallas_call(
-            functools.partial(scores_kernel, step, lambda x: room.place(x, size)),
+            functools.partial(
+                resident_scores if step else scores_kernel, step, lambda x: room.place(x, size)
+            ),
             out_shape=jax.ShapeDtypeStruct((classes, samples), jnp.float32),
-            in_specs=[SM] * 4 + [VM, in_hbm], out_specs=VM, compiler_params=SLOTS,
-            scratch_shapes=tile_room, name="scores",
+            in_specs=[SM] * 4 + [VM, VM if step else pl.BlockSpec(memory_space=pltpu.HBM)],
+            out_specs=VM, compiler_params=slots_params, name="scores",
+            scratch_shapes=[] if step else tile_room,
         )(*scalars, got, tiles)
         residual, loss = split_classify(step, n_cols, part, labels)
         losses.append(loss)
         grads = pl.pallas_call(
-            functools.partial(grads_kernel, step, lambda x: room.place(x, size)),
+            functools.partial(resident_grads, step, lambda x: room.place(x, size)),
             out_shape=spread,
-            in_specs=[SM] * 4 + [VM, in_hbm], out_specs=VM, compiler_params=SLOTS,
-            scratch_shapes=[pltpu.VMEM((room.spread, classes, size), jnp.float32), *tile_room],
+            in_specs=[SM] * 4 + [VM, VM], out_specs=VM, compiler_params=slots_params,
+            scratch_shapes=[pltpu.VMEM((room.spread, classes, size), jnp.float32)],
             name="grads",
         )(*scalars, residual, tiles)
         grads = pl.pallas_call(

time: 181 us -> 183 us (1.011); the launches traced: 177 us -> 183 us
  Pallas kernels: 175 us -> 180 us
    pallas_call x2, Pallas kernels: 60.5 us -> 65.9 us  [team_program(): pl.pallas_call(functools.partial(spread_kernel, room, n_rows), out_shape=...]
where the time goes in v3:
time: 183 us
  Pallas kernels  180 us (98%)
    pallas_call x2, Pallas kernels, team_program(): pl.pallas_call(functools.partial(spread_kernel, room, n_rows), out_shape=...  65.9 us
    pallas_call x2, Pallas kernels, team_program(): pl.pallas_call(functools.partial(gather_kernel, room, n_rows), out_shape=...  60 us
    pallas_call x1, Pallas kernels, mark(): pl.pallas_call(functools.partial(mark_kernel, n_rows, n_cols, steps), out...  14 us
    pallas_call x2, Pallas kernels, split_classify(): pl.pallas_call(functools.partial(split_classify_kernel, n_cols, step), ou...  13.6 us
    pallas_call x2, Pallas kernels, team_program(): pl.pallas_call(functools.partial(resident_scores if step else scores_kern...  8.93 us
    pallas_call x2, Pallas kernels, team_program(): pl.pallas_call(functools.partial(resident_grads, step, lambda x: room.pla...  6.4 us
    pallas_call x2, Pallas kernels, team_program(): pl.pallas_call(functools.partial(apply_pack_lists if more else apply_list...  6.39 us

profile of v3, /device:TPU:0, one launch (start us, length us, event | category | flops | bytes accessed | tf_op | source)
XLA Modules:
  0.0 182.6 jit_solution(6544034827405255009)
XLA Ops:
  0.6 14.0 %mark.1 = (bf16[4,8,16,128]{3,2,1,0:T(8,128)(2,1)}, s32[2,128]{1,0:T(2,128)}) custom-call(s32[2,128]{1,0:T(2,128)} %bitcast.22, s32[2]{0:T(128)} %bitcast.15), custom_call_target="tpu_custom_call" | custom-call | tf_op jit(solution)/shard_map/mark/pallas_call | solution.py:515
  14.6 2.4 %plan.1 = (s32[2,128]{1,0:T(2,128)S(1)}, s32[2,1152]{1,0:T(2,128)S(1)}, s32[1]{0:T(128)}) custom-call(bf16[4,8,16,128]{3,2,1,0:T(8,128)(2,1)} %get-tuple-element.205.all_hbm, s32[2,128]{1,0:T(2,128)} %get-tuple-element.206.cols_hbm), custom_call_target="tpu_custom_call" | custom-call | tf_op jit(solution)/shard_map/plan/pallas_call | solution.py:631
  17.6 165.0 %conditional.1 = (f32[32,16384]{1,0:T(8,128)}, f32[2,256]{1,0:T(2,128)}) conditional(s32[]{:T(128)} %bitcast.2, (s32[2,1152]{1,0:T(2,128)S(1)}, f32[32,16384]{1,0:T(8,128)}, s32[2,128]{1,0:T(2,128)S(1)}, s32[2,1,1,128]{3,2,1,0:T(1,128)}, f32[2,1,1,128]{3,2,1,0:T(1,128)}, /*index=5*/s32[2]{0:T(128)}, ...), branch_computations={%region_0.0_spmd, %region_1.0_spmd, %region_2.0_spmd, %region_3.0_... | conditional | flops 512 | bytes 101233016 | solution.py:1008
  17.9 0.0 slice-start.4
  17.9 2.6 %pack.8.send = bf16[170,32,128]{2,1,0:T(8,128)(2,1)S(1)} custom-call(s32[2,1152]{1,0:T(2,128)S(1)} %get-tuple-element.138.lists_ref, f32[32,16384]{1,0:T(8,128)} %get-tuple-element.140.weights_ref), custom_call_target="tpu_custom_call" | custom-call | tf_op jit(solution)/shard_map/cond/branch_2_fun/pack/pallas_call | solution.py:941
  20.5 0.0 copy-start.17
  20.5 0.0 copy-start.23
  20.5 0.0 copy-start.29
  20.5 34.1 %spread.16.recv_ref = bf16[224,32,128]{2,1,0:T(8,128)(2,1)S(1)} custom-call(bf16[170,32,128]{2,1,0:T(8,128)(2,1)S(1)} %pack.8.send), custom_call_target="tpu_custom_call" | custom-call | tf_op jit(solution)/shard_map/cond/branch_2_fun/spread/pallas_call | solution.py:947
  54.7 0.0 copy-start.11
  54.7 0.0 slice-start.5
  54.7 5.2 %scores.16.part_ref = f32[32,1024]{1,0:T(8,128)S(1)} custom-call(s32[2,128]{1,0:T(2,128)S(1)} %get-tuple-element.141.code_ref, s32[2,1,1,128]{3,2,1,0:T(1,128)S(1)} %copy-done.17, f32[2,1,1,128]{3,2,1,0:T(1,128)S(1)} %copy-done.23, s32[2]{0:T(128)S(1)} %copy-done.29, bf16[224,32,128]{2,1,0:T(8,128)(2,1)S(1)} %spread.16.recv_ref, ...), custom_call_target="tpu_custom_call" | custom-call | tf_op jit(solution)/shard_map/cond/branch_2_fun/scores/pallas_call | solution.py:952
  59.9 6.2 %classify.16 = (bf16[32,1024]{1,0:T(8,128)(2,1)S(1)}, f32[1,256]{1,0:T(1,128)S(1)}) custom-call(f32[32,1024]{1,0:T(8,128)S(1)} %scores.16.part_ref, s32[2,1024]{1,0:T(2,128)S(1)} %copy-done.11), custom_call_target="tpu_custom_call" | custom-call | tf_op jit(solution)/shard_map/cond/branch_2_fun/classify/pallas_call | solution.py:701
  66.1 3.2 %grads.16.grads_ref = bf16[224,32,128]{2,1,0:T(8,128)(2,1)S(1)} custom-call(s32[2,128]{1,0:T(2,128)S(1)} %get-tuple-element.141.code_ref, s32[2,1,1,128]{3,2,1,0:T(1,128)S(1)} %copy-done.17, f32[2,1,1,128]{3,2,1,0:T(1,128)S(1)} %copy-done.23, s32[2]{0:T(128)S(1)} %copy-done.29, bf16[32,1024]{1,0:T(8,128)(2,1)S(1)} %get-tuple-element.147.residual_ref, ...), custom_call_target="tpu_custom_call" | custom-call | tf_op jit(solution)/shard_map/cond/branch_2_fun/grads/pallas_call | solution.py:963
  69.3 0.0 copy-start.5
  69.4 29.9 %gather.16.grads_ref = bf16[170,32,128]{2,1,0:T(8,128)(2,1)S(1)} custom-call(bf16[224,32,128]{2,1,0:T(8,128)(2,1)S(1)} %grads.16.grads_ref), custom_call_target="tpu_custom_call" | custom-call | tf_op jit(solution)/shard_map/cond/branch_2_fun/gather/pallas_call | solution.py:970
  99.3 3.0 %apply.16 = (f32[32,16384]{1,0:T(8,128)S(1)}, bf16[170,32,128]{2,1,0:T(8,128)(2,1)S(1)}) custom-call(s32[2,1152]{1,0:T(2,128)S(1)} %get-tuple-element.138.lists_ref, f32[2]{0:T(128)S(1)} %copy-done.35, f32[32,16384]{1,0:T(8,128)S(1)} %copy-done.5, bf16[170,32,128]{2,1,0:T(8,128)(2,1)S(1)} %gather.16.grads_ref), custom_call_target="tpu_custom_call" | custom-call | tf_op jit(solution)/shard_map/cond/branch_2_fun/apply/pallas_call | solution.py:983
  102.3 31.8 %spread.17.recv_ref = bf16[224,32,128]{2,1,0:T(8,128)(2,1)S(1)} custom-call(bf16[170,32,128]{2,1,0:T(8,128)(2,1)S(1)} %get-tuple-element.149.send), custom_call_target="tpu_custom_call" | custom-call | tf_op jit(solution)/shard_map/cond/branch_2_fun/spread/pallas_call | solution.py:947
  134.1 3.8 %scores.17.part_ref = f32[32,1024]{1,0:T(8,128)S(1)} custom-call(s32[2,128]{1,0:T(2,128)S(1)} %get-tuple-element.141.code_ref, s32[2,1,1,128]{3,2,1,0:T(1,128)S(1)} %copy-done.17, f32[2,1,1,128]{3,2,1,0:T(1,128)S(1)} %copy-done.23, s32[2]{0:T(128)S(1)} %copy-done.29, bf16[224,32,128]{2,1,0:T(8,128)(2,1)S(1)} %spread.17.recv_ref, ...), custom_call_target="tpu_custom_call" | custom-call | tf_op jit(solution)/shard_map/cond/branch_2_fun/scores/pallas_call | solution.py:952
  137.8 7.4 %classify.17 = (bf16[32,1024]{1,0:T(8,128)(2,1)S(1)}, f32[1,256]{1,0:T(1,128)S(1)}) custom-call(f32[32,1024]{1,0:T(8,128)S(1)} %scores.17.part_ref, s32[2,1024]{1,0:T(2,128)S(1)} %copy-done.11), custom_call_target="tpu_custom_call" | custom-call | tf_op jit(solution)/shard_map/cond/branch_2_fun/classify/pallas_call | solution.py:701
  145.3 0.6 pad_maximum_fusion.2
  145.9 3.2 %grads.17.grads_ref = bf16[224,32,128]{2,1,0:T(8,128)(2,1)S(1)} custom-call(s32[2,128]{1,0:T(2,128)S(1)} %get-tuple-element.141.code_ref, s32[2,1,1,128]{3,2,1,0:T(1,128)S(1)} %copy-done.17, f32[2,1,1,128]{3,2,1,0:T(1,128)S(1)} %copy-done.23, s32[2]{0:T(128)S(1)} %copy-done.29, bf16[32,1024]{1,0:T(8,128)(2,1)S(1)} %get-tuple-element.150.residual_ref, ...), custom_call_target="tpu_custom_call" | custom-call | tf_op jit(solution)/shard_map/cond/branch_2_fun/grads/pallas_call | solution.py:963
  149.1 30.1 %gather.17.grads_ref = bf16[170,32,128]{2,1,0:T(8,128)(2,1)S(1)} custom-call(bf16[224,32,128]{2,1,0:T(8,128)(2,1)S(1)} %grads.17.grads_ref), custom_call_target="tpu_custom_call" | custom-call | tf_op jit(solution)/shard_map/cond/branch_2_fun/gather/pallas_call | solution.py:970
  179.2 3.4 %apply.17 = f32[32,16384]{1,0:T(8,128)} custom-call(s32[2,1152]{1,0:T(2,128)S(1)} %get-tuple-element.138.lists_ref, f32[2]{0:T(128)S(1)} %copy-done.35, f32[32,16384]{1,0:T(8,128)S(1)} %get-tuple-element.148.weights_ref, bf16[170,32,128]{2,1,0:T(8,128)(2,1)S(1)} %gather.17.grads_ref), custom_call_target="tpu_custom_call" | custom-call | tf_op jit(solution)/shard_map/cond/branch_2_fun/apply/pallas_call | solution.py:983
  (10 shorter events, 0.0 us)
Async XLA Ops:
  17.9 48.2 %slice-start.4 = ((s8[8388608]{0:T(1024)(128)(4,1)}), s8[4194304]{0:T(1024)(128)(4,1)S(1)}, s32[]{:S(2)}) async-start(s8[8388608]{0:T(1024)(128)(4,1)} %bitcast.7), calls=%async_computation.4 | async-start | bytes 8388608 | tf_op jit(solution)/shard_map/cond
  20.5 34.1 %copy-start.17 = (s32[2,1,1,128]{3,2,1,0:T(1,128)S(1)}, s32[2,1,1,128]{3,2,1,0:T(1,128)}, u32[]{:S(2)}) copy-start(s32[2,1,1,128]{3,2,1,0:T(1,128)} %get-tuple-element.142.row_ref) | copy-start | bytes 3076 | tf_op jit(solution)/shard_map/cond
  20.5 34.1 %copy-start.23 = (f32[2,1,1,128]{3,2,1,0:T(1,128)S(1)}, f32[2,1,1,128]{3,2,1,0:T(1,128)}, u32[]{:S(2)}) copy-start(f32[2,1,1,128]{3,2,1,0:T(1,128)} %get-tuple-element.143.scale_ref) | copy-start | bytes 3076 | tf_op jit(solution)/shard_map/cond
  20.5 34.1 %copy-start.29 = (s32[2]{0:T(128)S(1)}, s32[2]{0:T(128)}, u32[]{:S(2)}) copy-start(s32[2]{0:T(128)} %get-tuple-element.144.count_ref) | copy-start | bytes 28 | tf_op jit(solution)/shard_map/cond
  54.7 5.2 %copy-start.11 = (s32[2,1024]{1,0:T(2,128)S(1)}, s32[2,1024]{1,0:T(2,128)}, u32[]{:S(2)}) copy-start(s32[2,1024]{1,0:T(2,128)} %get-tuple-element.146.labels_ref) | copy-start | bytes 24580 | tf_op jit(solution)/shard_map/cond
  54.7 11.4 %slice-start.5 = ((s8[8388608]{0:T(1024)(128)(4,1)}), s8[4194304]{0:T(1024)(128)(4,1)S(1)}, s32[]{:S(2)}) async-start(s8[8388608]{0:T(1024)(128)(4,1)} %bitcast.7), calls=%async_computation.5 | async-start | bytes 8388608 | tf_op jit(solution)/shard_map/cond
  69.3 29.9 %copy-start.5 = (f32[32,16384]{1,0:T(8,128)S(1)}, f32[32,16384]{1,0:T(8,128)}, u32[]{:S(2)}) copy-start(f32[32,16384]{1,0:T(8,128)} %get-tuple-element.140.weights_ref) | copy-start | bytes 6291460 | tf_op jit(solution)/shard_map/cond
  69.3 29.9 %copy-start.35 = (f32[2]{0:T(128)S(1)}, f32[2]{0:T(128)}, u32[]{:S(2)}) copy-start(f32[2]{0:T(128)} %get-tuple-element.139.rate_ref) | copy-start | bytes 28 | tf_op jit(solution)/shard_map/cond
